TPU v7x, 32 devices: a whole 2x2x4 slice. The times are simulated.
32 devices in a mesh: wide: 8 (over z, x), narrow: 4 (over y, core).
Axes of the slice: x: 2, y: 2, z: 4, core: 2. Of those that a mesh axis runs over, the one named last changes fastest.
Arguments:
- points: bfloat16 [32768, 256], P('wide'), may hold values from -6 to 6
- q_init: float32 [16, 32768], P(None, 'wide'), may hold values from -80 to 80
- pairs: int32 [2, 2048], P(None, ('wide', 'narrow')), may hold values from 0 to 255, as said below
Outputs:
- basis: float32 [16, 32768], P(None, 'wide')
- coeffs: float32 [3, 2, 16, 16], replicated
Inputs may be any that keep to these rules, and one draw needn't show every extreme that they name: `pairs`: pair number g * 4 * 64 + m * 64 + o * 8 + c (g < 8, m < 4, o < 8, c < 8) has its first block in g * 32 .. (g + 1) * 32 - 1 and its second block in o * 32 .. (o + 1) * 32 - 1; the two ends of a pair differ.
All inputs are finite; a program needn't handle non-finite values.
Results may differ from a plain program's by a relative error of at most 0.0015.
Values may be sent and summed in bfloat16 or wider, within the bound.
A program may use at most 64 MiB of HBM per device.

v0:
```python
import functools

import jax
import jax.numpy as jnp
from jax import lax
from jax.experimental import pallas as pl
from jax.experimental.pallas import tpu as pltpu
from jax.sharding import PartitionSpec as P

BS = 128
STEPS = 3
LEVELS = 32767.0
KERNEL_FACTOR = 3.0
EPSILON = 1e-06
HIGH = lax.Precision.HIGHEST
MESH = pl.DeviceIdType.MESH


def unit_rows(points):
    wide32 = points.astype(jnp.float32)
    scaled = wide32 * lax.rsqrt(jnp.sum(wide32 * wide32, axis=-1, keepdims=True) + EPSILON)
    return scaled.astype(jnp.bfloat16)


def split(x):
    high = x.astype(jnp.bfloat16)
    return high, (x - high.astype(jnp.float32)).astype(jnp.bfloat16)


def coded(x, axes=1):
    top = jnp.maximum(jnp.max(jnp.abs(x), axis=axes, keepdims=True), 1e-30)
    scaled = jnp.clip(jnp.round(x * (LEVELS / top)), -LEVELS, LEVELS)
    return scaled.astype(jnp.int32).astype(jnp.int16), top * (1.0 / LEVELS)


def number(x):
    return x.astype(jnp.int32).astype(jnp.float32)


def dot32(a, b):
    return jnp.dot(a, b, precision=HIGH, preferred_element_type=jnp.float32)


def dot_nt(a, b, precision=None):
    return lax.dot_general(
        a, b, (((1,), (1,)), ((), ())), precision=precision, preferred_element_type=jnp.float32
    )


def tiles_kernel(capacity, me_ref, first_ref, unit_ref, second_ref, out_ref):
    d = pl.program_id(0)
    for c in range(capacity):
        s = dot_nt(unit_ref[first_ref[d * capacity + c]], second_ref[0, c])
        high, low = split(jnp.exp(KERNEL_FACTOR * (s - 1.0)))
        out_ref[c, :, :BS] = high
        out_ref[c, :, BS:] = low


def make_tiles(me, first, unit, second):
    wide_count, capacity, _, width = second.shape
    own_blocks = unit.shape[0]
    spec = pltpu.PrefetchScalarGridSpec(
        num_scalar_prefetch=2,
        grid=(wide_count,),
        in_specs=[
            pl.BlockSpec((own_blocks, BS, width), lambda d, m, f: (0, 0, 0)),
            pl.BlockSpec(
                (1, capacity, BS, width),
                lambda d, m, f: (lax.rem(m[0] - d + wide_count, wide_count), 0, 0, 0),
            ),
        ],
        out_specs=pl.BlockSpec((capacity, BS, 2 * BS), lambda d, m, f: (d, 0, 0)),
    )
    return pl.pallas_call(
        functools.partial(tiles_kernel, capacity),
        grid_spec=spec,
        out_shape=jax.ShapeDtypeStruct((wide_count * capacity, BS, 2 * BS), jnp.bfloat16),
        name="tiles",
    )(me, first, unit, second)


def factor_of(gram, r):
    i = lax.broadcasted_iota(jnp.int32, (r, r), 0)
    j = lax.broadcasted_iota(jnp.int32, (r, r), 1)
    both_i = lax.broadcasted_iota(jnp.int32, (r, 2 * r), 0)
    m = jnp.concatenate([gram, (i == j).astype(jnp.float32)], axis=1)
    lower = jnp.zeros((r, r), jnp.float32)
    for k in range(r):
        inv = 1.0 / jnp.sqrt(m[k : k + 1, k : k + 1])
        row = m[k : k + 1, :] * inv
        col = m[:, k : k + 1] * inv
        lower = jnp.where((j == k) & (i >= k), col, lower)
        m = jnp.where(both_i == k, row, jnp.where(both_i > k, m - col * row, m))
    upper = jnp.where(j >= i, m[:, :r], 0.0)
    inverse = jnp.where(j <= i, m[:, r:], 0.0)
    return lower, upper, inverse


def main_kernel(
    dims, first, local, owners, tiles, q_ref, out, coef,
    sb, rb, sb2, rq, ss, rs1, ss2, rs2, coded_blocks, scales, rb2, tf, pb, rs, ag, acc, out16, all16, psc, rsc, osc, asc, xs, blocks, prev, up, gs, gr,
    s1, r1, s2, r2, s3, r3, s4, r4, s5, r5, s6, r6, s7, r7, s8, r8, s9, r9,
):
    W, N, C, R, B, total = dims
    CR = C * R
    RN = R // N
    PR = RN * B
    me = lax.axis_index("wide")
    nar = lax.axis_index("narrow")

    def up_peer(d):
        return lax.rem(me + d, W)

    def down_peer(d):
        return lax.rem(me - d + W, W)

    barrier = pltpu.get_barrier_semaphore()
    for d in range(1, W):
        pl.semaphore_signal(barrier, inc=1, device_id={"wide": up_peer(d)}, device_id_type=MESH)
    for d in range(1, N):
        pl.semaphore_signal(
            barrier, inc=1, device_id={"narrow": lax.rem(nar + d, N)}, device_id_type=MESH
        )
    pl.semaphore_wait(barrier, W - 1 + N - 1)

    def request(d):
        rows = pl.ds(d * CR, CR)
        return pltpu.make_async_remote_copy(
            src_ref=sb.at[rows], dst_ref=rb.at[rows], send_sem=s1.at[d], recv_sem=r1.at[d],
            device_id={"wide": up_peer(d)}, device_id_type=MESH,
        )

    def answer(d):
        rows = pl.ds(d * CR, CR)
        return pltpu.make_async_remote_copy(
            src_ref=sb2.at[rows], dst_ref=rq.at[rows], send_sem=s2.at[d], recv_sem=r2.at[d],
            device_id={"wide": down_peer(d)}, device_id_type=MESH,
        )

    def request_scale(d):
        rows = pl.ds(d * R, R)
        return pltpu.make_async_remote_copy(
            src_ref=ss.at[rows], dst_ref=rs1.at[rows], send_sem=s6.at[d], recv_sem=r6.at[d],
            device_id={"wide": up_peer(d)}, device_id_type=MESH,
        )

    def answer_scale(d):
        rows = pl.ds(d * R, R)
        return pltpu.make_async_remote_copy(
            src_ref=ss2.at[rows], dst_ref=rs2.at[rows], send_sem=s7.at[d], recv_sem=r7.at[d],
            device_id={"wide": down_peer(d)}, device_id_type=MESH,
        )

    lane = lax.broadcasted_iota(jnp.int32, (R, BS), 1)

    def scatter(d):
        return pltpu.make_async_remote_copy(
            src_ref=pb.at[pl.ds(lax.rem(nar + d, N) * PR, PR)], dst_ref=rs.at[d],
            send_sem=s3.at[d], recv_sem=r3.at[d],
            device_id={"narrow": lax.rem(nar + d, N)}, device_id_type=MESH,
        )

    def gather(d):
        mine = pl.ds(nar * PR, PR)
        return pltpu.make_async_remote_copy(
            src_ref=out16, dst_ref=all16.at[mine], send_sem=s4.at[d], recv_sem=r4.at[d],
            device_id={"narrow": lax.rem(nar + d, N)}, device_id_type=MESH,
        )

    def gathered(d):
        theirs = pl.ds(lax.rem(nar - d + N, N) * PR, PR)
        return pltpu.make_async_remote_copy(
            src_ref=out16, dst_ref=all16.at[theirs], send_sem=s4.at[d], recv_sem=r4.at[d],
            device_id={"narrow": lax.rem(nar + d, N)}, device_id_type=MESH,
        )

    def scatter_scale(d):
        return pltpu.make_async_remote_copy(
            src_ref=psc.at[d], dst_ref=rsc.at[d], send_sem=s8.at[d], recv_sem=r8.at[d],
            device_id={"narrow": lax.rem(nar + d, N)}, device_id_type=MESH,
        )

    def gather_scale(d, slot):
        return pltpu.make_async_remote_copy(
            src_ref=osc, dst_ref=asc.at[slot], send_sem=s9.at[d], recv_sem=r9.at[d],
            device_id={"narrow": lax.rem(nar + d, N)}, device_id_type=MESH,
        )

    lane8 = lax.broadcasted_iota(jnp.int32, (8, BS), 1)

    def gram_copy(d):
        return pltpu.make_async_remote_copy(
            src_ref=gs, dst_ref=gr.at[d], send_sem=s5.at[d], recv_sem=r5.at[d],
            device_id={"wide": up_peer(d)}, device_id_type=MESH,
        )

    def gram_sum(value):
        gs[:, : 2 * R] = value
        gr[0, :, : 2 * R] = value
        for d in range(1, W):
            gram_copy(d).start()
        for d in range(1, W):
            gram_copy(d).wait_recv()
        summed = jnp.zeros((2 * R, 2 * R), jnp.float32)
        for s in range(W):
            summed += gr[lax.rem(me - s + W, W)][:, : 2 * R]
        for d in range(1, W):
            gram_copy(d).wait_send()
        return summed / total

    gs[...] = jnp.zeros_like(gs)
    xs[:R, :] = q_ref[...]
    xs[R:, :] = jnp.zeros((R, B * BS), jnp.float32)
    prev[...] = jnp.zeros_like(prev)
    up[...] = jnp.zeros_like(up)
    start = gram_sum(dot_nt(xs[...], xs[...], HIGH))
    _, _, inverse0 = factor_of(start[:R, :R], R)
    xs[:R, :] = dot32(inverse0, q_ref[...])

    def step(k, carry):
        for b in range(B):
            value = xs[:R, b * BS : (b + 1) * BS]
            blocks[b] = value
            whole, unit_of = coded(value)
            coded_blocks[b] = whole
            scales[b] = jnp.broadcast_to(unit_of, (R, BS))
        for d in range(W):
            spread = jnp.zeros((R, BS), jnp.float32)
            for c in range(C):
                value = coded_blocks[local[d * C + c]]
                (rb if d == 0 else sb)[pl.ds((d * C + c) * R, R), :] = value
                spread = jnp.where(lane == c, scales[local[d * C + c]], spread)
            (rs1 if d == 0 else ss)[pl.ds(d * R, R), :] = spread
            if d:
                request(d).start()
                request_scale(d).start()

        def group(d, carry):
            @pl.when(d > 0)
            def _():
                request(d).wait_recv()
                request_scale(d).wait_recv()

            scale_rows = pl.ds(pl.multiple_of(d * R, R), R)
            scale = rs1[scale_rows, :]
            spread = jnp.zeros((R, BS), jnp.float32)
            for c in range(C):
                p = d * C + c
                rows = pl.ds(pl.multiple_of(p * R, R), R)
                tile = tiles[p]
                high, low = split(number(rb[rows, :]))
                left = jnp.concatenate(
                    [
                        jnp.concatenate([high, high], axis=1),
                        jnp.concatenate([low, jnp.zeros_like(low)], axis=1),
                    ],
                    axis=0,
                )
                both = dot_nt(left, tile)
                tf[rows, :] = (both[:R] + both[R:]) * scale[:, c : c + 1]
                high, low = split(blocks[first[p]])
                both = jnp.dot(
                    jnp.concatenate([high, low], axis=0), tile, preferred_element_type=jnp.float32
                )
                whole, unit_of = coded(both[:R, :BS] + both[R:, :BS] + both[:R, BS:])
                sb2[rows, :] = whole
                spread = jnp.where(lane == c, unit_of, spread)
            ss2[scale_rows, :] = spread

            @pl.when(d > 0)
            def _():
                answer(d).start()
                answer_scale(d).start()

            return carry

        lax.fori_loop(0, W, group, 0)
        for d in range(W):
            if d:
                answer(d).wait_recv()
                answer_scale(d).wait_recv()
            scale = (rs2 if d else ss2)[pl.ds(d * R, R), :]
            for c in range(C):
                rows = pl.ds((d * C + c) * R, R)
                rb2[rows, :] = number((rq if d else sb2)[rows, :]) * scale[:, c : c + 1]

        one_hot = owners[...]
        for n in range(1, N + 1):
            part = lax.rem(nar + n, N)
            spread = jnp.zeros((8, BS), jnp.float32)
            for q in range(RN):
                r = part * RN + q
                x = jnp.concatenate(
                    [tf[pl.ds(r, W * C, stride=R), :], rb2[pl.ds(r, W * C, stride=R), :]], axis=0
                )
                high, low = split(x)
                value = jnp.dot(
                    one_hot,
                    jnp.concatenate([high, low], axis=0),
                    preferred_element_type=jnp.float32,
                )
                if n == N:
                    acc[pl.ds(q * B, B), :] = value
                else:
                    whole, unit_of = coded(value, (0, 1))
                    pb[pl.ds(pl.multiple_of(part * PR + q * B, B), B), :] = whole
                    spread = jnp.where(lane8 == q, unit_of, spread)
            if n < N:
                psc[n] = spread
                scatter(n).start()
                scatter_scale(n).start()
        for d in range(1, N):
            scatter(d).wait_recv()
            scatter_scale(d).wait_recv()
        spread = jnp.zeros((8, BS), jnp.float32)
        for q in range(RN):
            rows = pl.ds(q * B, B)
            value = acc[rows, :]
            for d in range(1, N):
                value += number(rs[d, rows, :]) * rsc[d][:1, q : q + 1]
            whole, unit_of = coded(value, (0, 1))
            out16[rows, :] = whole
            all16[pl.ds(pl.multiple_of(nar * PR + q * B, B), B), :] = whole
            spread = jnp.where(lane8 == q, unit_of, spread)
        osc[...] = spread
        asc[nar] = spread
        for d in range(1, N):
            gather(d).start()
            gather_scale(d, nar).start()
        for d in range(1, N):
            gathered(d).wait_recv()
            gather_scale(d, lax.rem(nar - d + N, N)).wait_recv()
        for r in range(R):
            rows = pl.ds(r * B, B)
            unit_of = asc[r // RN][:1, r % RN : r % RN + 1]
            ag[rows, :] = number(all16[rows, :]) * unit_of

        for b in range(B):
            xs[R:, b * BS : (b + 1) * BS] = ag[pl.ds(b, R, stride=B), :]
        xs[R:, :] = xs[R:, :] - dot32(up[...], prev[...])
        summed = gram_sum(dot_nt(xs[...], xs[...], HIGH))
        basis_gram = summed[:R, :R]
        along = summed[:R, R:]
        along_t = summed[R:, :R]
        raw = summed[R:, R:]
        gram = raw - 2.0 * dot32(along_t, along) + dot32(along_t, dot32(basis_gram, along))
        lower, upper, inverse = factor_of(gram, R)
        coef[k, 0] = along
        coef[k, 1] = lower
        prev[...] = xs[:R, :]
        up[...] = upper
        mix = jnp.concatenate([-dot32(inverse, along_t), inverse], axis=1)
        xs[:R, :] = dot32(mix, xs[...])

        for d in range(1, W):
            request(d).wait_send()
            answer(d).wait_send()
            request_scale(d).wait_send()
            answer_scale(d).wait_send()
        for d in range(1, N):
            scatter(d).wait_send()
            gather(d).wait_send()
            scatter_scale(d).wait_send()
            gather_scale(d, nar).wait_send()
        return carry

    lax.fori_loop(0, STEPS, step, 0)
    out[...] = xs[:R, :]


def spread_kernel(dims, first, second, asked, unit, tiles, *scratch):
    W, N, C, B = dims
    Z = W // 2
    reach = Z - 1
    bufs = (scratch[:reach], scratch[reach : 2 * reach])
    out_buf, in_buf, sz, rz, sy, ry, sc, rc, sx, rx = scratch[2 * reach :]
    me = lax.axis_index("wide")
    nar = lax.axis_index("narrow")
    z, x = lax.div(me, 2), lax.rem(me, 2)
    across = me + 1 - 2 * x
    over = lax.rem(nar + 2, N)
    core = nar + 1 - 2 * lax.rem(nar, 2)
    core_over = lax.rem(core + 2, N)
    BQ = B // N

    def valid(t, g):
        return (z >= t) if g == 0 else (z + t < Z)

    def room(g):
        return (z + 1 < Z) if g == 0 else (z > 0)

    def held(t, g):
        return unit if t == 0 else bufs[g][t - 1]

    def quarter(ref, q):
        return ref.at[pl.ds(q * BQ, BQ)]

    def remote(src, dst, send, recv, where):
        return pltpu.make_async_remote_copy(
            src_ref=src, dst_ref=dst, send_sem=send, recv_sem=recv,
            device_id=where, device_id_type=MESH,
        )

    def along(t, g):
        return remote(
            quarter(held(t, g), nar), quarter(held(t + 1, g), nar),
            sz.at[g, t], rz.at[g, t + 1], {"wide": me + 2 if g == 0 else me - 2},
        )

    def arrived(t, g):
        part = quarter(held(t, g), nar)
        return remote(
            part, part, sz.at[g, t - 1], rz.at[g, t], {"wide": me + 2 if g == 0 else me - 2}
        )

    def sideways(t, g, q):
        part = quarter(held(t, g), q)
        return remote(part, part, sy.at[g, t], ry.at[g, t], {"narrow": over})

    def inside(t, g, j, q):
        part = quarter(held(t, g), q)
        return remote(part, part, sc.at[j, g, t], rc.at[j, g, t], {"narrow": core})

    def place(t, g):
        return g * reach + t

    def cross(t, g):
        k = place(t, g)
        return remote(out_buf.at[k], in_buf.at[k], sx.at[k], rx.at[k], {"wide": across})

    def group_of(t, g):
        return z - t if g == 0 else z + t

    def serve(t, g):
        o = 2 * group_of(t, g) + x
        for c in range(C):
            out_buf[place(t, g), c] = held(t, g)[asked[o * C + c]]
        cross(t, g).start()

    def make(o, load):
        slot = lax.rem(me - o + W, W)
        for c in range(C):
            s = dot_nt(unit[first[slot * C + c]], load(o, c))
            high, low = split(jnp.exp(KERNEL_FACTOR * (s - 1.0)))
            tiles[slot * C + c, :, :BS] = high
            tiles[slot * C + c, :, BS:] = low

    def near_tiles(t, g):
        make(2 * group_of(t, g) + x, lambda o, c: held(t, g)[second[o * C + c]])

    def far_tiles(t, g):
        cross(t, g).wait_recv()
        make(2 * group_of(t, g) + 1 - x, lambda o, c: in_buf[place(t, g), c])

    barrier = pltpu.get_barrier_semaphore()
    for where in ({"wide": across}, {"narrow": over}, {"narrow": core}):
        pl.semaphore_signal(barrier, inc=1, device_id=where, device_id_type=MESH)
    for g in range(2):
        @pl.when(room(g))
        def _():
            pl.semaphore_signal(
                barrier, inc=1, device_id={"wide": me + 2 if g == 0 else me - 2},
                device_id_type=MESH,
            )
    pl.semaphore_wait(barrier, 3 + jnp.minimum(z, 1) + jnp.minimum(Z - 1 - z, 1))

    for g in range(2):
        @pl.when(room(g))
        def _():
            along(0, g).start()
    serve(0, 0)
    near_tiles(0, 0)

    for t in range(1, Z + 1):
        if t < Z:
            for g in range(2):
                @pl.when(valid(t, g))
                def _():
                    arrived(t, g).wait_recv()

                    @pl.when(room(g))
                    def _():
                        if t + 1 < Z:
                            along(t, g).start()

                    sideways(t, g, nar).start()
                    inside(t, g, 0, nar).start()
        if t > 1:
            for g in range(2):
                @pl.when(valid(t - 1, g))
                def _():
                    sideways(t - 1, g, over).wait_recv()
                    inside(t - 1, g, 1, over).start()
                    inside(t - 1, g, 0, core).wait_recv()
                    inside(t - 1, g, 1, core_over).wait_recv()
                    serve(t - 1, g)
            for g in range(2):
                @pl.when(valid(t - 1, g))
                def _():
                    near_tiles(t - 1, g)
            if t == 2:
                far_tiles(0, 0)
    for t in range(1, Z):
        for g in range(2):
            @pl.when(valid(t, g))
            def _():
                far_tiles(t, g)

    cross(0, 0).wait_send()
    for t in range(Z):
        for g in range(2):
            if t:
                @pl.when(valid(t, g))
                def _():
                    sideways(t, g, nar).wait_send()
                    inside(t, g, 0, nar).wait_send()
                    inside(t, g, 1, over).wait_send()
                    cross(t, g).wait_send()

            if t + 1 < Z:
                @pl.when(valid(t, g) & room(g))
                def _():
                    along(t, g).wait_send()


def spread_tiles(first, second, asked, unit, wide_count, narrow_count):
    own_blocks, _, width = unit.shape
    pair_count = first.shape[0]
    C = pair_count // wide_count
    Z = wide_count // 2
    vmem = pl.BlockSpec(memory_space=pltpu.VMEM)
    smem = pl.BlockSpec(memory_space=pltpu.SMEM)
    half = pltpu.SemaphoreType.DMA((2, Z))
    full = pltpu.SemaphoreType.DMA((2, 2, Z))
    flat = pltpu.SemaphoreType.DMA((2 * Z - 1,))
    ends = pltpu.VMEM((2 * Z - 1, C, BS, width), jnp.bfloat16)
    return pl.pallas_call(
        functools.partial(spread_kernel, (wide_count, narrow_count, C, own_blocks)),
        out_shape=jax.ShapeDtypeStruct((pair_count, BS, 2 * BS), jnp.bfloat16),
        in_specs=[smem, smem, smem, vmem],
        out_specs=vmem,
        scratch_shapes=[pltpu.VMEM(unit.shape, jnp.bfloat16)] * (2 * Z - 2)
        + [ends, ends, half, half, half, half, full, full, flat, flat],
        compiler_params=pltpu.CompilerParams(collective_id=1, has_side_effects=True),
        name="spread",
    )(first, second, asked, unit)


SPREAD_BYTES = 16 * 2**20


def lanczos(first, local, owners, tiles, q_init, wide_count, narrow_count, total):
    R, cols = q_init.shape
    B = cols // BS
    pair_count = first.shape[0]
    C = pair_count // wide_count
    dims = (wide_count, narrow_count, C, R, B, total)
    vmem = pl.BlockSpec(memory_space=pltpu.VMEM)
    smem = pl.BlockSpec(memory_space=pltpu.SMEM)
    f32 = jnp.float32
    pairs_buf = pltpu.VMEM((pair_count * R, BS), f32)
    coded_buf = pltpu.VMEM((pair_count * R, BS), jnp.int16)
    scale_buf = pltpu.VMEM((wide_count * R, BS), f32)
    part = R // narrow_count * B
    wide_sem = pltpu.SemaphoreType.DMA((wide_count,))
    narrow_sem = pltpu.SemaphoreType.DMA((narrow_count,))
    return pl.pallas_call(
        functools.partial(main_kernel, dims),
        out_shape=(
            jax.ShapeDtypeStruct((R, cols), f32),
            jax.ShapeDtypeStruct((STEPS, 2, R, R), f32),
        ),
        in_specs=[smem, smem, vmem, vmem, vmem],
        out_specs=(vmem, vmem),
        scratch_shapes=[
            coded_buf, coded_buf, coded_buf, coded_buf,
            scale_buf, scale_buf, scale_buf, scale_buf,
            pltpu.VMEM((B, R, BS), jnp.int16),
            pltpu.VMEM((B, R, BS), f32),
            pairs_buf, pairs_buf,
            pltpu.VMEM((R * B, BS), jnp.int16),
            pltpu.VMEM((narrow_count, part, BS), jnp.int16),
            pltpu.VMEM((R * B, BS), f32),
            pltpu.VMEM((part, BS), f32),
            pltpu.VMEM((part, BS), jnp.int16),
            pltpu.VMEM((R * B, BS), jnp.int16),
            pltpu.VMEM((narrow_count, 8, BS), f32),
            pltpu.VMEM((narrow_count, 8, BS), f32),
            pltpu.VMEM((8, BS), f32),
            pltpu.VMEM((narrow_count, 8, BS), f32),
            pltpu.VMEM((2 * R, cols), f32),
            pltpu.VMEM((B, R, BS), f32),
            pltpu.VMEM((R, cols), f32),
            pltpu.VMEM((R, R), f32),
            pltpu.VMEM((2 * R, BS), f32),
            pltpu.VMEM((wide_count, 2 * R, BS), f32),
            wide_sem, wide_sem, wide_sem, wide_sem,
            narrow_sem, narrow_sem, narrow_sem, narrow_sem,
            wide_sem, wide_sem, wide_sem, wide_sem, wide_sem, wide_sem,
            narrow_sem, narrow_sem, narrow_sem, narrow_sem,
        ],
        compiler_params=pltpu.CompilerParams(collective_id=0, has_side_effects=True),
        name="lanczos",
    )(first, local, owners, tiles, q_init)


def per_device(points, q_init, pairs):
    wide_count = lax.axis_size("wide")
    narrow_count = lax.axis_size("narrow")
    me = lax.axis_index("wide")
    own_blocks = points.shape[0] // BS
    width = points.shape[1]
    pair_count = pairs.shape[1]
    capacity = pair_count // wide_count
    total = own_blocks * BS * wide_count
    unit = unit_rows(points).reshape(own_blocks, BS, width)
    turn = jnp.arange(wide_count, dtype=jnp.int32)
    first_rows = (pairs[0] - me * own_blocks).reshape(wide_count, capacity)
    first = first_rows[(me - turn) % wide_count].reshape(pair_count)
    second = (pairs[1].reshape(wide_count, capacity) - turn[:, None] * own_blocks)
    every = lax.all_to_all(
        jnp.broadcast_to(second.reshape(1, pair_count), (wide_count, pair_count)),
        "wide", split_axis=0, concat_axis=0, tiled=True,
    ).reshape(wide_count, wide_count, capacity)
    local_ids = lax.dynamic_index_in_dim(every, me, axis=1, keepdims=False)
    local = local_ids[(me + turn) % wide_count].reshape(pair_count)
    targets = jnp.concatenate([first, local, first, local])
    owners = (jnp.arange(own_blocks, dtype=jnp.int32)[:, None] == targets[None, :]).astype(
        jnp.bfloat16
    )
    buffers = (wide_count - 2) * unit.size * 2
    if wide_count % 2 == 0 and wide_count > 2 and narrow_count == 4 and buffers <= SPREAD_BYTES:
        asked = lax.dynamic_index_in_dim(every, me + 1 - 2 * (me % 2), axis=0, keepdims=False)
        tiles = spread_tiles(
            first, second.reshape(pair_count), asked.reshape(pair_count), unit,
            wide_count, narrow_count,
        )
    else:
        blocks = lax.all_to_all(
            unit[local_ids.reshape(pair_count)], "wide", split_axis=0, concat_axis=0, tiled=True
        ).reshape(wide_count, capacity, BS, width)
        tiles = make_tiles(jnp.reshape(me, (1,)).astype(jnp.int32), first, unit, blocks)
    return lanczos(first, local, owners, tiles, q_init, wide_count, narrow_count, total)


def solution(mesh):
    placed = (P("wide", None), P(None, "wide"), P(None, ("wide", "narrow")))
    return jax.shard_map(
        per_device, mesh=mesh, in_specs=placed, out_specs=(P(None, "wide"), P()), check_vma=False
    )
```

profile of v0, /device:TPU:0, one launch (start us, length us, event | category | flops | bytes accessed | tf_op | source)
XLA Modules:
  0.0 208.7 jit_solution(14898750855892094826)
XLA Ops:
  0.6 0.1 sub.51
  0.7 0.1 sub.52
  0.8 0.8 subtract_bitcast_fusion
  1.6 0.6 broadcast_in_dim.2
  2.2 7.3 %all-to-all-start = ((s32[8,1,64]{2,1,0:T(1,128)}), s32[8,1,64]{2,1,0:T(1,128)S(1)}, u32[]{:S(2)}, u32[]{:S(2)}) async-start(s32[8,1,64]{2,1,0:T(1,128)} %broadcast_in_dim.2), calls=%async_computation | async-start | bytes 8192 | tf_op jit(solution)/shard_map/all_to_all | solution.py:621
  9.5 0.1 sub.55
  9.5 1.2 bitcast_subtract_fusion.second
  10.8 2.2 %fusion = f32[4096]{0:T(1024)S(1)} fusion(bf16[4096,256]{1,0:T(8,128)(2,1)} %param.3), kind=kLoop, calls=%fused_computation.4 | loop fusion | flops 3141632 | bytes 2113536 | tf_op jit(solution)/shard_map/reduce_sum | solution.py:21
  13.0 2.9 %fusion.1 = bf16[4096,256]{1,0:T(8,128)(2,1)} fusion(bf16[4096,256]{1,0:T(8,128)(2,1)} %param.3, f32[4096]{0:T(1024)S(1)} %add_rsqrt_fusion), kind=kLoop, calls=%fused_computation.5 | loop fusion | flops 3145728 | bytes 4210688 | tf_op jit(solution)/shard_map/convert_element_type | solution.py:22
  15.9 0.1 sub.48
  16.0 0.6 gather_fusion
  16.6 0.1 reshape.148.first
  16.7 0.0 copy-start
  16.7 0.0 all-to-all-done
  16.7 0.5 broadcast.165
  17.2 0.7 reduce.7
  17.9 0.1 reshape.149
  17.9 0.7 reshape.151.asked
  18.6 0.6 gather_fusion.1
  19.2 0.1 reshape.150.local
  19.2 0.0 copy-start.1
  19.2 0.1 pad_add_fusion
  19.3 0.6 fusion.2.owners
  19.9 0.0 copy-done
  19.9 69.3 %spread.1.tiles = bf16[64,128,256]{2,1,0:T(8,128)(2,1)} custom-call(s32[64]{0:T(128)} %copy-done, s32[64]{0:T(128)} %bitcast_subtract_fusion.second, s32[64]{0:T(128)} %reshape.151.asked, bf16[32,128,256]{2,1,0:T(8,128)(2,1)} %bitcast.10), custom_call_target="tpu_custom_call" | custom-call | tf_op jit(solution)/shard_map/spread/pallas_call | solution.py:537
  89.3 0.0 copy-done.1
  89.3 116.3 %lanczos.1 = (f32[16,4096]{1,0:T(8,128)}, f32[3,2,16,16]{3,2,1,0:T(8,128)}) custom-call(s32[64]{0:T(128)} %copy-done, s32[64]{0:T(128)} %copy-done.1, bf16[32,256]{1,0:T(8,128)(2,1)} %fusion.2.owners, bf16[64,128,256]{2,1,0:T(8,128)(2,1)} %spread.1.tiles, f32[16,4096]{1,0:T(8,128)} %q_ref.1), custom_call_target="tpu_custom_call" | custom-call | tf_op jit(solution)/shard_map/lanczos/pallas_call | solution.py:567
  205.6 1.7 copy.7
  207.2 1.4 copy.8
  (7 shorter events, 0.0 us)
Async XLA Ops:
  2.2 14.5 %all-to-all-start = ((s32[8,1,64]{2,1,0:T(1,128)}), s32[8,1,64]{2,1,0:T(1,128)S(1)}, u32[]{:S(2)}, u32[]{:S(2)}) async-start(s32[8,1,64]{2,1,0:T(1,128)} %broadcast_in_dim.2), calls=%async_computation | async-start | bytes 8192 | tf_op jit(solution)/shard_map/all_to_all | solution.py:621
  16.7 3.3 %copy-start = (s32[64]{0:T(128)}, s32[64]{0:T(128)S(1)}, u32[]{:S(2)}) copy-start(s32[64]{0:T(128)S(1)} %reshape.148.first) | copy-start | bytes 772
  19.2 70.1 %copy-start.1 = (s32[64]{0:T(128)}, s32[64]{0:T(128)S(1)}, u32[]{:S(2)}) copy-start(s32[64]{0:T(128)S(1)} %reshape.150.local) | copy-start | bytes 772
where the time goes:
time: 209 us
  Pallas kernels  186 us (89%)
  other arithmetic  8.54 us (4%)
  starting transfers between devices  7.28 us (3%)
  local copies, waits for them, and re-layouts  6.52 us (3%)
    pallas_call x1, Pallas kernels, lanczos(): pl.pallas_call(functools.partial(main_kernel, dims), out_shape=(jax.Shape...  116 us
    pallas_call x1, Pallas kernels, spread_tiles(): pl.pallas_call(functools.partial(spread_kernel, (wide_count, narrow_count...  69.3 us
    all_to_all x1, starting transfers between devices, per_device(): lax.all_to_all(jnp.broadcast_to(second.reshape(1, pair_count), (wide_coun...  7.28 us
  transfers between devices with their start and end apart: 1, of which 0 were waited for; matrix products, arithmetic and copies ran while one was open for 3% of the time, Pallas kernels for 0%

commit v1 on v0

--- a/solution.py
+++ b/solution.py
@@ -12,6 +12,7 @@
 LEVELS = 32767.0
 KERNEL_FACTOR = 3.0
 EPSILON = 1e-06
+LOG_STEPS = 256.0
 HIGH = lax.Precision.HIGHEST
 MESH = pl.DeviceIdType.MESH
 
@@ -368,185 +369,621 @@
     out[...] = xs[:R, :]
 
 
-def spread_kernel(dims, first, second, asked, unit, tiles, *scratch):
-    W, N, C, B = dims
-    Z = W // 2
-    reach = Z - 1
-    bufs = (scratch[:reach], scratch[reach : 2 * reach])
-    out_buf, in_buf, sz, rz, sy, ry, sc, rc, sx, rx = scratch[2 * reach :]
+def quarter_scale(code):
+    return jnp.exp(code.astype(jnp.float32) * (1.0 / LOG_STEPS))
+
+
+def packed(values):
+    top = jnp.abs(values[0])
+    for value in values[1:]:
+        top = jnp.maximum(top, jnp.abs(value))
+    top = jnp.maximum(jnp.max(top, axis=1, keepdims=True), 1e-30)
+    whole = jnp.ceil(jnp.log(top) * LOG_STEPS).astype(jnp.int32)
+    whole = jnp.broadcast_to(whole, values[0].shape)
+    factor = LEVELS / quarter_scale(whole)
+    out = [
+        jnp.clip(jnp.round(value * factor), -LEVELS, LEVELS).astype(jnp.int32).astype(jnp.int16)
+        for value in values
+    ]
+    return out + [whole.astype(jnp.int16)]
+
+
+SLOTS = 5
+Z_ROWS = 48
+PARTS = 4
+
+
+def fused_kernel(dims, names, points, q_ref, pairs_ref, out, coef, *refs):
+    W, N, C, R, B, F, total = dims
+    s_ = dict(zip(names, refs))
+    (unit, uq0, uq1, uq2, uq3, uq4, kt, tf1, tf2, vo, vr, rep, perm, shift, yt, zt, oht1, oht2, oh1, oh2, lv, ls, idx_i, idx_j, n2, w2, o1n, o1w, i1n, i1w,
+     y1, y2, gs, gn, gt, gw, fin, qc, pv, wp, zp, at, inv, up) = (s_[n] for n in DATA)
+    sem = s_
+    uq = (uq0, uq1, uq2, uq3, uq4)
+    QR = BS // N
+    JQ = B // N
+    HALF = W * C
     me = lax.axis_index("wide")
     nar = lax.axis_index("narrow")
     z, x = lax.div(me, 2), lax.rem(me, 2)
-    across = me + 1 - 2 * x
-    over = lax.rem(nar + 2, N)
-    core = nar + 1 - 2 * lax.rem(nar, 2)
-    core_over = lax.rem(core + 2, N)
-    BQ = B // N
-
-    def valid(t, g):
-        return (z >= t) if g == 0 else (z + t < Z)
-
-    def room(g):
-        return (z + 1 < Z) if g == 0 else (z > 0)
-
-    def held(t, g):
-        return unit if t == 0 else bufs[g][t - 1]
-
-    def quarter(ref, q):
-        return ref.at[pl.ds(q * BQ, BQ)]
-
-    def remote(src, dst, send, recv, where):
+    h = lax.div(z, 2)
+    e = lax.rem(z, 2)
+    cd = (1 - h) * (3 - z) + h * (z - 2)
+    cs = (1 - h) * (z + 2) + h * (3 - z)
+    ax = 1 - x
+    side = z + 1 - 2 * e
+    XN = 2 * z + ax
+    SRC = [XN, 2 * cs + x, 2 * cs + ax, 2 * side + (1 - e) * ax + e * x]
+    DST = [XN, 2 * cd + x, 2 * cd + ax, 2 * side + (1 - e) * x + e * ax]
+    GROUP = [me] + SRC
+    lane = lax.broadcasted_iota(jnp.int32, (R, BS), 1)
+    lane8 = lax.broadcasted_iota(jnp.int32, (8, BS), 1)
+    sub8 = lax.broadcasted_iota(jnp.int32, (8, BS), 0)
+
+    def slot_is(s, lanes=None):
+        lanes = lane if lanes is None else lanes
+        return (lanes >= s * QR) & (lanes < s * QR + QR)
+
+    def filled(value):
+        value = value + pltpu.roll(value, QR, 1)
+        return value + pltpu.roll(value, 2 * QR, 1)
+
+    def remote(src, dst, name, at_, where):
         return pltpu.make_async_remote_copy(
-            src_ref=src, dst_ref=dst, send_sem=send, recv_sem=recv,
+            src_ref=src, dst_ref=dst, send_sem=sem["s_" + name].at[at_], recv_sem=sem["r_" + name].at[at_],
             device_id=where, device_id_type=MESH,
         )
 
-    def along(t, g):
-        return remote(
-            quarter(held(t, g), nar), quarter(held(t + 1, g), nar),
-            sz.at[g, t], rz.at[g, t + 1], {"wide": me + 2 if g == 0 else me - 2},
-        )
-
-    def arrived(t, g):
-        part = quarter(held(t, g), nar)
-        return remote(
-            part, part, sz.at[g, t - 1], rz.at[g, t], {"wide": me + 2 if g == 0 else me - 2}
-        )
-
-    def sideways(t, g, q):
-        part = quarter(held(t, g), q)
-        return remote(part, part, sy.at[g, t], ry.at[g, t], {"narrow": over})
-
-    def inside(t, g, j, q):
-        part = quarter(held(t, g), q)
-        return remote(part, part, sc.at[j, g, t], rc.at[j, g, t], {"narrow": core})
-
-    def place(t, g):
-        return g * reach + t
-
-    def cross(t, g):
-        k = place(t, g)
-        return remote(out_buf.at[k], in_buf.at[k], sx.at[k], rx.at[k], {"wide": across})
-
-    def group_of(t, g):
-        return z - t if g == 0 else z + t
-
-    def serve(t, g):
-        o = 2 * group_of(t, g) + x
-        for c in range(C):
-            out_buf[place(t, g), c] = held(t, g)[asked[o * C + c]]
-        cross(t, g).start()
-
-    def make(o, load):
-        slot = lax.rem(me - o + W, W)
-        for c in range(C):
-            s = dot_nt(unit[first[slot * C + c]], load(o, c))
-            high, low = split(jnp.exp(KERNEL_FACTOR * (s - 1.0)))
-            tiles[slot * C + c, :, :BS] = high
-            tiles[slot * C + c, :, BS:] = low
-
-    def near_tiles(t, g):
-        make(2 * group_of(t, g) + x, lambda o, c: held(t, g)[second[o * C + c]])
-
-    def far_tiles(t, g):
-        cross(t, g).wait_recv()
-        make(2 * group_of(t, g) + 1 - x, lambda o, c: in_buf[place(t, g), c])
+    def wide(d):
+        return {"wide": d}
+
+    def nearby(d):
+        return {"narrow": lax.rem(nar + d, N)}
+
+    def behind(d):
+        return lax.rem(nar - d + N, N)
+
+    PART = B // PARTS
+
+    def part(s, t):
+        return uq[s].at[pl.ds(t * PART, PART)]
+
+    def hop_x(t):
+        return remote(part(0, t), part(1, t), "px", t, wide(XN))
+
+    def hop_c(t):
+        return remote(part(0, t), part(2, t), "pc", t, wide(DST[1]))
+
+    def hop_f(t):
+        return remote(part(2, t), part(3, t), "pf", t, wide(XN))
+
+    def hop_a(t, s=0):
+        return remote(part(s, t), part(4, t), "pa", t, wide(2 * side + x))
+
+    def list_near(d):
+        return remote(pairs_ref, lv.at[0, nar], "ln", d, nearby(d))
+
+    def list_wide(d):
+        return remote(lv.at[0], lv.at[d], "lw", d, wide(DST[d]))
+
+    def vec_near(k, d):
+        return remote(n2.at[k, nar], n2.at[k, nar], "vn", (k, d), nearby(d))
+
+    def vec_near_in(k, d):
+        place = n2.at[k, behind(d)]
+        return remote(place, place, "vn", (k, d), nearby(d))
+
+    def vec_wide(k, d):
+        return remote(n2.at[k, nar], w2.at[k, d], "vw", (k, d), wide(DST[d]))
+
+    def sum_near(k, d):
+        return remote(o1n.at[k, d], i1n.at[k, d], "sn", (k, d), nearby(d))
+
+    def sum_wide(k, d):
+        return remote(o1w.at[k, d], i1w.at[k, d], "sw", (k, d), wide(SRC[d]))
+
+    def gram_near(k, d):
+        return remote(gs.at[k], gn.at[k, nar], "gn", (k, d), nearby(d))
+
+    def gram_near_in(k, d):
+        place = gn.at[k, behind(d)]
+        return remote(place, place, "gn", (k, d), nearby(d))
+
+    def gram_wide(k, d):
+        return remote(gt.at[k], gw.at[k, me], "gw", (k, d), wide(lax.rem(me + d, W)))
+
+    def gram_wide_in(k, d):
+        place = gw.at[k, lax.rem(me - d + W, W)]
+        return remote(place, place, "gw", (k, d), wide(lax.rem(me + d, W)))
+
+    def fin_near(d):
+        return remote(fin.at[nar], fin.at[nar], "fn", d, nearby(d))
+
+    def fin_near_in(d):
+        place = fin.at[behind(d)]
+        return remote(place, place, "fn", d, nearby(d))
 
     barrier = pltpu.get_barrier_semaphore()
-    for where in ({"wide": across}, {"narrow": over}, {"narrow": core}):
-        pl.semaphore_signal(barrier, inc=1, device_id=where, device_id_type=MESH)
-    for g in range(2):
-        @pl.when(room(g))
+    for d in range(1, W):
+        pl.semaphore_signal(barrier, inc=1, device_id=wide(lax.rem(me + d, W)), device_id_type=MESH)
+    for d in range(1, N):
+        pl.semaphore_signal(barrier, inc=1, device_id=nearby(d), device_id_type=MESH)
+
+    def normalise(b, carry):
+        unit[b] = unit_rows(points[pl.ds(pl.multiple_of(b * BS, BS), BS), :])
+        return carry
+
+    def quarter(b, carry):
+        uq0[b] = unit_rows(points[pl.ds(pl.multiple_of(b * BS + nar * QR, QR), QR), :])
+        return carry
+
+    lax.fori_loop(0, B, quarter, 0, unroll=4)
+
+    def square(x_):
+        four = jnp.concatenate([x_] * (BS // (2 * R)), axis=0)
+        full = dot_nt(x_, four, HIGH)
+        small = jnp.zeros((8, BS), jnp.float32)
+        for a in range(2 * R // 8):
+            small = jnp.where(slot_is(a, lane8), full[8 * a : 8 * a + 8], small)
+        return small
+
+    def gram_value(k):
+        total_ = gw[k, 0]
+        for d in range(1, W):
+            total_ = total_ + gw[k, d]
+        rows = [total_] + [pltpu.roll(total_, BS - a * 2 * R, 1) for a in range(1, 2 * R // 8)]
+        return jnp.concatenate(rows, axis=0)[:, : 2 * R] / total
+
+    def gram_send(k):
+        gw[k, me] = gt[k]
+        for d in range(1, W):
+            gram_wide(k, d).start()
+
+    def gram_collect(k):
+        for d in range(1, N):
+            gram_near_in(k, d).wait_recv()
+        value = gn[k, 0]
+        for d in range(1, N):
+            value = value + gn[k, d]
+        gt[k] = value
+        gram_send(k)
+
+    def gram_start(k):
+        value = square(jnp.concatenate([qc[...], wp[...]], axis=0))
+        gs[k] = value
+        gn[k, nar] = value
+        for d in range(1, N):
+            gram_near(k, d).start()
+
+    def gram_finish(k):
+        for d in range(1, W):
+            gram_wide_in(k, d).wait_recv()
+        summed = gram_value(k)
+        along = summed[:R, R:]
+        along_t = summed[R:, :R]
+        gram = summed[R:, R:] - 2.0 * dot32(along_t, along) + dot32(along_t, dot32(summed[:R, :R], along))
+        lower, upper, inverse = factor_of(gram, R)
+        coef[k - 1, 0] = along
+        coef[k - 1, 1] = lower
+        at[...] = along_t
+        inv[...] = inverse
+        up[...] = upper
+        pv[...] = qc[...]
+        qc[...] = dot32(inverse, wp[...] - dot32(along_t, qc[...]))
+
+    pl.semaphore_wait(barrier, W - 1 + N - 1)
+
+    for t in range(PARTS):
+        hop_x(t).start()
+        hop_c(t).start()
+
+        @pl.when(e == 0)
         def _():
-            pl.semaphore_signal(
-                barrier, inc=1, device_id={"wide": me + 2 if g == 0 else me - 2},
-                device_id_type=MESH,
+            hop_a(t).start()
+
+    lv[0, nar] = pairs_ref[...]
+    for d in range(1, N):
+        list_near(d).start()
+    q_all = q_ref[...]
+    gt[0] = square(jnp.concatenate([q_all, q_all], axis=0))
+    gram_send(0)
+    lax.fori_loop(0, B, normalise, 0, unroll=2)
+
+    def places(rows, columns, of):
+        row = lax.broadcasted_iota(jnp.int32, (rows, columns), 0)
+        column = lax.broadcasted_iota(jnp.int32, (rows, columns), 1)
+        return (row == of(column)).astype(jnp.float32).astype(jnp.bfloat16)
+
+    rep[...] = places(BS, N * BS, lambda l: (l // BS) * QR + (l & (QR - 1)))
+    perm[...] = places(
+        N * BS, N * BS, lambda l: ((l // QR) & (N - 1)) * BS + (l // BS) * QR + (l & (QR - 1))
+    )
+    for a in range(N):
+        shift[a * BS : (a + 1) * BS, :] = places(
+            BS, BS, lambda l: ((l // QR + N - a) & (N - 1)) * QR + (l & (QR - 1))
+        )
+
+    for d in range(1, N):
+        place = lv.at[0, behind(d)]
+        remote(place, place, "ln", d, nearby(d)).wait_recv()
+    for d in range(1, 4):
+        list_wide(d).start()
+
+    for jq in range(JQ):
+        value = jnp.zeros((R, BS), jnp.float32)
+        for s in range(N):
+            b = N * jq + s
+            one = filled(jnp.where(slot_is(nar), q_ref[:, b * BS : (b + 1) * BS], 0.0))
+            value = jnp.where(slot_is(s), one, value)
+        wp[:, jq * BS : (jq + 1) * BS] = value
+
+    for d in range(1, W):
+        gram_wide_in(0, d).wait_recv()
+    _, _, inverse0 = factor_of(gram_value(0)[:R, :R], R)
+    qc[...] = dot32(inverse0, wp[...])
+    for ref in (pv, zp, at, up):
+        ref[...] = jnp.zeros_like(ref)
+    inv[...] = (
+        lax.broadcasted_iota(jnp.int32, (R, R), 0) == lax.broadcasted_iota(jnp.int32, (R, R), 1)
+    ).astype(jnp.float32)
+
+    def lanes_of(ref):
+        return [ref[:, jq * BS : (jq + 1) * BS] for jq in range(JQ)]
+
+    def vec_send(k, ref):
+        for jq, value in enumerate(packed(lanes_of(ref))):
+            n2[k, nar, jq * R : (jq + 1) * R, :] = value
+        for d in range(1, N):
+            vec_near(k, d).start()
+        for d in range(4):
+            vec_wide(k, d).start()
+
+    vec_send(0, qc)
+
+    for d in range(1, 4):
+        remote(lv.at[d], lv.at[d], "lw", d, wide(DST[d])).wait_recv()
+    local = pltpu.make_async_copy(lv, ls, sem["m_ls"])
+    local.start()
+    local.wait()
+
+    kinds = []
+    for s in range(SLOTS):
+        kinds.append((s, 0))
+        if s > 1:
+            kinds.append((s, 1))
+
+    for at_kind, (s, kind) in enumerate(kinds):
+        other = GROUP[s]
+
+        def indices(mq, carry):
+            ch = at_kind * N + mq
+            vi = jnp.zeros((8, BS), jnp.int32)
+            vj = jnp.zeros((8, BS), jnp.int32)
+            for c in range(C):
+                if kind == 0:
+                    i = ls[0, mq, 0, other * C + c]
+                    j = ls[0, mq, 0, HALF + other * C + c]
+                else:
+                    j = ls[s - 1, mq, 0, me * C + c]
+                    i = ls[s - 1, mq, 0, HALF + me * C + c]
+                idx_i[ch * C + c] = i
+                idx_j[ch * C + c] = j
+                vi = jnp.where(sub8 == c, i, vi)
+                vj = jnp.where(sub8 == c, j, vj)
+            rows = pl.ds(pl.multiple_of(ch * C, C), C)
+            row = (vi & (N - 1)) * JQ + vi // N
+            oht1[rows, :] = (row == lane8).astype(jnp.float32)
+            row = ((vj + N - (sub8 & (N - 1))) & (N - 1)) * Z_ROWS + s * JQ + vj // N
+            oht2[rows, :BS] = (row == lane8).astype(jnp.float32)
+            oht2[rows, BS:] = (row == lane8 + BS).astype(jnp.float32)
+            return carry
+
+        lax.fori_loop(0, N, indices, 0)
+
+    turned = jnp.transpose(oht1[...])[: oh1.shape[0]].astype(jnp.bfloat16)
+    oh1[...] = jnp.concatenate([turned, turned], axis=1)
+    turned = jnp.transpose(oht2[...])[: oh2.shape[0]].astype(jnp.bfloat16)
+    oh2[...] = jnp.concatenate([turned, turned], axis=1)
+
+    def tiles_of(want):
+        for at_kind, (s, kind) in enumerate(kinds):
+            if s != want:
+                continue
+
+            def make(mq, carry):
+                ch = at_kind * N + mq
+                for c in range(C):
+                    p = ch * C + c
+                    sim = dot_nt(uq[s][idx_j[p]], unit[idx_i[p]])
+                    high, low = split(jnp.exp(KERNEL_FACTOR * (sim - 1.0)))
+                    rows = pl.ds(pl.multiple_of(p * QR, QR), QR)
+                    kt[rows, :BS] = high
+                    kt[rows, BS:] = low
+                return carry
+
+            lax.fori_loop(0, N, make, 0)
+
+    tiles_of(0)
+    for t in range(PARTS):
+        hop_x(t).wait_recv()
+
+        @pl.when(e == 1)
+        def _():
+            hop_a(t, 1).start()
+
+        hop_c(t).wait_recv()
+        hop_f(t).start()
+    tiles_of(1)
+    tiles_of(2)
+    for t in range(PARTS):
+        hop_a(t).wait_recv()
+    tiles_of(4)
+    for t in range(PARTS):
+        hop_f(t).wait_recv()
+    tiles_of(3)
+
+    chunks = len(kinds) * N
+    slots_of_chunk = [s for s, _ in kinds for _ in range(N)]
+
+    def unpacked(ref, k, d):
+        scale = quarter_scale(ref[k, d, JQ * R : (JQ + 1) * R, :].astype(jnp.int32)) * (1.0 / LEVELS)
+        return [number(ref[k, d, jq * R : (jq + 1) * R, :]) * scale for jq in range(JQ)]
+
+    def both(value):
+        return jnp.concatenate(split(value), axis=0)
+
+    def scatter(tf, one_hot, keep):
+        for r in range(0, R, 2):
+            columns = []
+            for q in range(2):
+                high, low = split(tf[pl.ds(r + q, chunks * C, stride=R), :])
+                columns.append(jnp.concatenate([high, low], axis=0))
+            value = jnp.dot(
+                one_hot[...], jnp.concatenate(columns, axis=1), preferred_element_type=jnp.float32
             )
-    pl.semaphore_wait(barrier, 3 + jnp.minimum(z, 1) + jnp.minimum(Z - 1 - z, 1))
-
-    for g in range(2):
-        @pl.when(room(g))
+            keep(r, value[:, :BS])
+            keep(r + 1, value[:, BS:])
+
+    def moved(value, matrix):
+        rows = value.shape[0]
+        value = jnp.dot(both(value), matrix[...], preferred_element_type=jnp.float32)
+        return value[:rows] + value[rows:]
+
+    def step(k, carry):
+        for d in range(1, N):
+            vec_near_in(k, d).wait_recv()
+        quarters = [unpacked(n2, k, q) for q in range(N)]
+        pieces = [
+            jnp.concatenate([both(quarters[q][jq]) for q in range(N)], axis=1) for jq in range(JQ)
+        ]
+        value = jnp.dot(jnp.concatenate(pieces, axis=0), perm[...], preferred_element_type=jnp.float32)
+        value = value.astype(jnp.bfloat16)
+        for jq in range(JQ):
+            for s in range(N):
+                vo[jq * N + s] = value[2 * R * jq : 2 * R * (jq + 1), s * BS : (s + 1) * BS]
+        mine = unpacked(n2, k, nar)
+
+        def keep_remote(s, values):
+            value = jnp.dot(
+                jnp.concatenate([both(v) for v in values], axis=0), rep[...],
+                preferred_element_type=jnp.float32,
+            ).astype(jnp.bfloat16)
+            for jq in range(JQ):
+                for b in range(N):
+                    vr[s * B + jq * N + b] = value[2 * R * jq : 2 * R * (jq + 1), b * BS : (b + 1) * BS]
+
+        keep_remote(0, mine)
+
+        @pl.when(k > 0)
         def _():
-            along(0, g).start()
-    serve(0, 0)
-    near_tiles(0, 0)
-
-    for t in range(1, Z + 1):
-        if t < Z:
-            for g in range(2):
-                @pl.when(valid(t, g))
-                def _():
-                    arrived(t, g).wait_recv()
-
-                    @pl.when(room(g))
-                    def _():
-                        if t + 1 < Z:
-                            along(t, g).start()
-
-                    sideways(t, g, nar).start()
-                    inside(t, g, 0, nar).start()
-        if t > 1:
-            for g in range(2):
-                @pl.when(valid(t - 1, g))
-                def _():
-                    sideways(t - 1, g, over).wait_recv()
-                    inside(t - 1, g, 1, over).start()
-                    inside(t - 1, g, 0, core).wait_recv()
-                    inside(t - 1, g, 1, core_over).wait_recv()
-                    serve(t - 1, g)
-            for g in range(2):
-                @pl.when(valid(t - 1, g))
-                def _():
-                    near_tiles(t - 1, g)
-            if t == 2:
-                far_tiles(0, 0)
-    for t in range(1, Z):
-        for g in range(2):
-            @pl.when(valid(t, g))
-            def _():
-                far_tiles(t, g)
-
-    cross(0, 0).wait_send()
-    for t in range(Z):
-        for g in range(2):
-            if t:
-                @pl.when(valid(t, g))
-                def _():
-                    sideways(t, g, nar).wait_send()
-                    inside(t, g, 0, nar).wait_send()
-                    inside(t, g, 1, over).wait_send()
-                    cross(t, g).wait_send()
-
-            if t + 1 < Z:
-                @pl.when(valid(t, g) & room(g))
-                def _():
-                    along(t, g).wait_send()
-
-
-def spread_tiles(first, second, asked, unit, wide_count, narrow_count):
-    own_blocks, _, width = unit.shape
-    pair_count = first.shape[0]
-    C = pair_count // wide_count
-    Z = wide_count // 2
+            gram_collect(k)
+
+        def second(ch, carry):
+            left = jnp.concatenate([vo[idx_i[ch * C + c]] for c in range(C)], axis=0)
+            tile = kt[pl.ds(pl.multiple_of(ch * C * QR, C * QR), C * QR), :]
+            full = dot_nt(jnp.concatenate([left, left], axis=1), tile)
+            for c in range(C):
+                columns = slice((c // N) * BS, (c // N + 1) * BS)
+                value = full[2 * R * c : 2 * R * c + R, columns] + full[2 * R * c + R : 2 * R * (c + 1), columns]
+                value = jnp.where(slot_is(c % N), value, 0.0)
+                tf2[pl.ds(pl.multiple_of((ch * C + c) * R, R), R), :] = value
+            return carry
+
+        lax.fori_loop(0, chunks, second, 0, unroll=2)
+
+        def keep2(r, value):
+            for a in range(N):
+                zt[r * SLOTS * JQ : (r + 1) * SLOTS * JQ, a * BS : (a + 1) * BS] = (
+                    value[a * Z_ROWS : a * Z_ROWS + SLOTS * JQ]
+                )
+
+        scatter(tf2, oh2, keep2)
+        batch = R // 4
+        for first_r in range(0, R, batch):
+            value = moved(zt[first_r * SLOTS * JQ : (first_r + batch) * SLOTS * JQ, :], shift)
+            for r in range(batch):
+                for s in range(SLOTS):
+                    place = (r * SLOTS + s) * JQ
+                    y2[s, pl.ds(first_r + r, JQ, stride=R), :] = value[place : place + JQ]
+        for d in range(4):
+            for jq, value in enumerate(packed([y2[d + 1, jq * R : (jq + 1) * R, :] for jq in range(JQ)])):
+                o1w[k, d, jq * R : (jq + 1) * R, :] = value
+            sum_wide(k, d).start()
+
+        for d in range(4):
+            remote(w2.at[k, d], w2.at[k, d], "vw", (k, d), wide(DST[d])).wait_recv()
+            keep_remote(d + 1, unpacked(w2, k, d))
+
+        for s in range(SLOTS):
+            first_chunk = slots_of_chunk.index(s)
+
+            def first(ch, carry):
+                left = []
+                for c in range(C):
+                    value = vr[s * B + idx_j[ch * C + c]]
+                    value = jnp.where(slot_is(c % N, lane2), value, jnp.zeros_like(value))
+                    pieces = [jnp.zeros_like(value)] * (C // N)
+                    pieces[c // N] = value
+                    left.append(jnp.concatenate(pieces, axis=1))
+                tile = kt[pl.ds(pl.multiple_of(ch * C * QR, C * QR), C * QR), :]
+                full = jnp.dot(jnp.concatenate(left, axis=0), tile, preferred_element_type=jnp.float32)
+                for c in range(C):
+                    high = full[2 * R * c : 2 * R * c + R]
+                    low = full[2 * R * c + R : 2 * R * (c + 1)]
+                    tf1[pl.ds(pl.multiple_of((ch * C + c) * R, R), R), :] = (
+                        high[:, :BS] + high[:, BS:] + low[:, :BS]
+                    )
+                return carry
+
+            lax.fori_loop(first_chunk, first_chunk + slots_of_chunk.count(s), first, 0, unroll=2)
+
+        def keep1(r, value):
+            for s in range(N):
+                yt[r * JQ : (r + 1) * JQ, s * BS : (s + 1) * BS] = value[s * JQ : (s + 1) * JQ]
+
+        scatter(tf1, oh1, keep1)
+        value = moved(yt[...], perm)
+        for r in range(R):
+            for q in range(N):
+                y1[q, pl.ds(r, JQ, stride=R), :] = value[r * JQ : (r + 1) * JQ, q * BS : (q + 1) * BS]
+
+        for d in range(1, N):
+            to = lax.rem(nar + d, N)
+            for jq, value in enumerate(packed([y1[to, jq * R : (jq + 1) * R, :] for jq in range(JQ)])):
+                o1n[k, d, jq * R : (jq + 1) * R, :] = value
+            sum_near(k, d).start()
+
+        @pl.when(k > 0)
+        def _():
+            gram_finish(k)
+
+        image = [y1[nar, jq * R : (jq + 1) * R, :] + y2[0, jq * R : (jq + 1) * R, :] for jq in range(JQ)]
+        for d in range(4):
+            sum_wide(k, d).wait_recv()
+            image = [a + b for a, b in zip(image, unpacked(i1w, k, d))]
+        for d in range(1, N):
+            sum_near(k, d).wait_recv()
+            image = [a + b for a, b in zip(image, unpacked(i1n, k, d))]
+        image = jnp.concatenate(image, axis=1)
+        image = dot32(inv[...], image - dot32(at[...], zp[...]))
+        zp[...] = image
+        wp[...] = image - dot32(up[...], pv[...])
+
+        @pl.when(k < STEPS - 1)
+        def _():
+            vec_send(k + 1, wp)
+
+        gram_start(k + 1)
+        return carry
+
+    lane2 = lax.broadcasted_iota(jnp.int32, (2 * R, BS), 1)
+    lax.fori_loop(0, STEPS, step, 0)
+    gram_collect(STEPS)
+    gram_finish(STEPS)
+    for jq, value in enumerate(lanes_of(qc)):
+        fin[nar, jq * R : (jq + 1) * R, :] = value
+    for d in range(1, N):
+        fin_near(d).start()
+    for d in range(1, N):
+        fin_near_in(d).wait_recv()
+    value = moved(jnp.concatenate([fin[q] for q in range(N)], axis=1), perm)
+    for jq in range(JQ):
+        for s in range(N):
+            b = jq * N + s
+            out[:, b * BS : (b + 1) * BS] = value[jq * R : (jq + 1) * R, s * BS : (s + 1) * BS]
+
+    for t in range(PARTS):
+        hop_x(t).wait_send()
+        hop_c(t).wait_send()
+        hop_a(t).wait_send()
+        hop_f(t).wait_send()
+    for d in range(1, N):
+        list_near(d).wait_send()
+        fin_near(d).wait_send()
+    for d in range(1, 4):
+        list_wide(d).wait_send()
+    for d in range(1, W):
+        gram_wide(0, d).wait_send()
+    for k in range(STEPS):
+        for d in range(1, N):
+            vec_near(k, d).wait_send()
+            sum_near(k, d).wait_send()
+            gram_near(k + 1, d).wait_send()
+        for d in range(4):
+            vec_wide(k, d).wait_send()
+            sum_wide(k, d).wait_send()
+        for d in range(1, W):
+            gram_wide(k + 1, d).wait_send()
+
+
+DATA = (
+    "unit", "uq0", "uq1", "uq2", "uq3", "uq4", "kt", "tf1", "tf2", "vo", "vr", "rep", "perm", "shift", "yt", "zt", "oht1", "oht2",
+    "oh1", "oh2", "lv", "ls", "idx_i", "idx_j", "n2", "w2", "o1n", "o1w", "i1n", "i1w", "y1", "y2",
+    "gs", "gn", "gt", "gw", "fin", "qc", "pv", "wp", "zp", "at", "inv", "up",
+)
+
+
+def fused(points, q_init, pairs, W, N):
+    R, cols = q_init.shape
+    F = points.shape[1]
+    B = cols // BS
+    pair_count = pairs.shape[1]
+    C = pair_count // W
+    QR, JQ = BS // N, B // N
+    P_ = (SLOTS + SLOTS - 2) * N * C
+    f32, bf16, i16, i32 = jnp.float32, jnp.bfloat16, jnp.int16, jnp.int32
+    V = pltpu.VMEM
+    message = ((JQ + 1) * R, BS)
+    rounds = STEPS + 1
+    columns = JQ * BS
+    shapes = {
+        "unit": V((B, BS, F), bf16), **{f"uq{s}": V((B, QR, F), bf16) for s in range(SLOTS)}, "kt": V((P_ * QR, 2 * BS), bf16),
+        "tf1": V((P_ * R, BS), f32), "tf2": V((P_ * R, BS), f32),
+        "vo": V((B, 2 * R, BS), bf16), "vr": V((SLOTS * B, 2 * R, BS), bf16),
+        "oht1": V((P_, BS), f32), "oht2": V((P_, 2 * BS), f32),
+        "rep": V((BS, N * BS), bf16), "perm": V((N * BS, N * BS), bf16), "shift": V((N * BS, BS), bf16),
+        "yt": V((R * JQ, N * BS), f32), "zt": V((R * SLOTS * JQ, N * BS), f32),
+        "oh1": V((B, 2 * P_), bf16), "oh2": V((N * Z_ROWS, 2 * P_), bf16),
+        "lv": V((4, N, 1, 2 * pair_count), i32), "ls": pltpu.SMEM((4, N, 1, 2 * pair_count), i32),
+        "idx_i": pltpu.SMEM((P_,), i32), "idx_j": pltpu.SMEM((P_,), i32),
+        "n2": V((STEPS, N) + message, i16), "w2": V((STEPS, 4) + message, i16),
+        "o1n": V((STEPS, N) + message, i16), "o1w": V((STEPS, 4) + message, i16),
+        "i1n": V((STEPS, N) + message, i16), "i1w": V((STEPS, 4) + message, i16),
+        "y1": V((N, JQ * R, BS), f32), "y2": V((SLOTS, JQ * R, BS), f32),
+        "gs": V((rounds, 8, BS), f32), "gn": V((rounds, N, 8, BS), f32),
+        "gt": V((rounds, 8, BS), f32), "gw": V((rounds, W, 8, BS), f32),
+        "fin": V((N, JQ * R, BS), f32),
+        "qc": V((R, columns), f32), "pv": V((R, columns), f32), "wp": V((R, columns), f32),
+        "zp": V((R, columns), f32),
+        "at": V((R, R), f32), "inv": V((R, R), f32), "up": V((R, R), f32),
+    }
+    sems = {
+        "px": (PARTS,), "pc": (PARTS,), "pf": (PARTS,), "pa": (PARTS,), "ln": (N,), "lw": (4,),
+        "vn": (STEPS, N), "vw": (STEPS, 4), "sn": (STEPS, N), "sw": (STEPS, 4),
+        "gn": (rounds, N), "gw": (rounds, W), "fn": (N,),
+    }
+    names = list(DATA)
+    scratch = [shapes[n] for n in DATA]
+    for name, shape in sems.items():
+        for way in "sr":
+            names.append(way + "_" + name)
+            scratch.append(pltpu.SemaphoreType.DMA(shape))
+    names.append("m_ls")
+    scratch.append(pltpu.SemaphoreType.DMA)
     vmem = pl.BlockSpec(memory_space=pltpu.VMEM)
-    smem = pl.BlockSpec(memory_space=pltpu.SMEM)
-    half = pltpu.SemaphoreType.DMA((2, Z))
-    full = pltpu.SemaphoreType.DMA((2, 2, Z))
-    flat = pltpu.SemaphoreType.DMA((2 * Z - 1,))
-    ends = pltpu.VMEM((2 * Z - 1, C, BS, width), jnp.bfloat16)
+    dims = (W, N, C, R, B, F, B * BS * W)
     return pl.pallas_call(
-        functools.partial(spread_kernel, (wide_count, narrow_count, C, own_blocks)),
-        out_shape=jax.ShapeDtypeStruct((pair_count, BS, 2 * BS), jnp.bfloat16),
-        in_specs=[smem, smem, smem, vmem],
-        out_specs=vmem,
-        scratch_shapes=[pltpu.VMEM(unit.shape, jnp.bfloat16)] * (2 * Z - 2)
-        + [ends, ends, half, half, half, half, full, full, flat, flat],
+        functools.partial(fused_kernel, dims, tuple(names)),
+        out_shape=(
+            jax.ShapeDtypeStruct((R, cols), f32),
+            jax.ShapeDtypeStruct((STEPS, 2, R, R), f32),
+        ),
+        in_specs=[vmem, vmem, vmem],
+        out_specs=(vmem, vmem),
+        scratch_shapes=scratch,
         compiler_params=pltpu.CompilerParams(collective_id=1, has_side_effects=True),
-        name="spread",
-    )(first, second, asked, unit)
-
-
-SPREAD_BYTES = 16 * 2**20
+        name="fused",
+    )(points, q_init, lax.rem(pairs, B).reshape(1, 2 * pair_count))
 
 
 def lanczos(first, local, owners, tiles, q_init, wide_count, narrow_count, total):
@@ -612,6 +1049,8 @@
     width = points.shape[1]
     pair_count = pairs.shape[1]
     capacity = pair_count // wide_count
+    if wide_count == 8 and narrow_count == 4 and own_blocks == 8 * narrow_count and capacity == 8:
+        return fused(points, q_init, pairs, wide_count, narrow_count)
     total = own_blocks * BS * wide_count
     unit = unit_rows(points).reshape(own_blocks, BS, width)
     turn = jnp.arange(wide_count, dtype=jnp.int32)
@@ -628,18 +1067,10 @@
     owners = (jnp.arange(own_blocks, dtype=jnp.int32)[:, None] == targets[None, :]).astype(
         jnp.bfloat16
     )
-    buffers = (wide_count - 2) * unit.size * 2
-    if wide_count % 2 == 0 and wide_count > 2 and narrow_count == 4 and buffers <= SPREAD_BYTES:
-        asked = lax.dynamic_index_in_dim(every, me + 1 - 2 * (me % 2), axis=0, keepdims=False)
-        tiles = spread_tiles(
-            first, second.reshape(pair_count), asked.reshape(pair_count), unit,
-            wide_count, narrow_count,
-        )
-    else:
-        blocks = lax.all_to_all(
-            unit[local_ids.reshape(pair_count)], "wide", split_axis=0, concat_axis=0, tiled=True
-        ).reshape(wide_count, capacity, BS, width)
-        tiles = make_tiles(jnp.reshape(me, (1,)).astype(jnp.int32), first, unit, blocks)
+    blocks = lax.all_to_all(
+        unit[local_ids.reshape(pair_count)], "wide", split_axis=0, concat_axis=0, tiled=True
+    ).reshape(wide_count, capacity, BS, width)
+    tiles = make_tiles(jnp.reshape(me, (1,)).astype(jnp.int32), first, unit, blocks)
     return lanczos(first, local, owners, tiles, q_init, wide_count, narrow_count, total)
 
 

time: 209 us -> 135 us (0.65)
  Pallas kernels: 186 us -> 129 us
  other arithmetic: 8.54 us -> 0.69 us
  starting transfers between devices: 7.28 us -> 0 us
  local copies, waits for them, and re-layouts: 6.52 us -> 3.68 us
    pallas_call x2 -> x1, Pallas kernels: 186 us -> 129 us  [fused(): pl.pallas_call(functools.partial(fused_kernel, dims, tuple(names)), out_s...]
    all_to_all x1 -> x0, starting transfers between devices: 7.28 us -> none  [per_device(): lax.all_to_all(jnp.broadcast_to(second.reshape(1, pair_count), (wide_coun...]
    convert_element_type x2 -> x0, other arithmetic: 3.56 us -> none  [the longest x1 2.94 us: unit_rows(): return scaled.astype(jnp.bfloat16)]
    reduce_sum x1 -> x0, other arithmetic: 2.21 us -> none  [unit_rows(): jnp.sum(wide32 * wide32, axis=-1, keepdims=True) + EPSILON]
  transfers between devices with their start and end apart: 1 -> 0, of which waited for: 0 -> 0; matrix products, arithmetic and copies ran while one was open for 3% -> 0% of each run, Pallas kernels for 0% -> 0%
where the time goes in v1:
time: 135 us; the launch traced here: 134 us
  Pallas kernels  129 us (96%)
  local copies, waits for them, and re-layouts  3.68 us (3%)
    pallas_call x1, Pallas kernels, fused(): pl.pallas_call(functools.partial(fused_kernel, dims, tuple(names)), out_s...  129 us
    unnamed x2, local copies, waits for them, and re-layouts  3.09 us

profile of v1, /device:TPU:0, one launch (start us, length us, event | category | flops | bytes accessed | tf_op | source)
XLA Modules:
  0.0 134.5 jit_solution(2032168075250711259)
XLA Ops:
  0.6 0.7 compare_select_fusion
  1.3 0.6 reshape.7.pairs_ref
  1.9 129.5 %fused.1 = (f32[16,4096]{1,0:T(8,128)}, f32[3,2,16,16]{3,2,1,0:T(8,128)}) custom-call(bf16[4096,256]{1,0:T(8,128)(2,1)} %points.1, f32[16,4096]{1,0:T(8,128)} %q_ref.1, s32[1,128]{1,0:T(1,128)} %reshape.7.pairs_ref), custom_call_target="tpu_custom_call" | custom-call | tf_op jit(solution)/shard_map/fused/pallas_call | solution.py:975
  131.4 1.7 %copy.7 = f32[16,4096]{1,0:T(8,128)} copy(f32[16,4096]{1,0:T(8,128)} %get-tuple-element.4) | data formatting | bytes 524288
  133.1 1.4 %copy.8 = f32[3,2,16,16]{3,2,1,0:T(8,128)} copy(f32[3,2,16,16]{3,2,1,0:T(8,128)} %get-tuple-element.5) | data formatting | bytes 12288

commit v2 on v1

--- a/solution.py
+++ b/solution.py
@@ -571,22 +571,41 @@
         pv[...] = qc[...]
         qc[...] = dot32(inverse, wp[...] - dot32(along_t, qc[...]))
 
+    lv[0, nar] = pairs_ref[...]
+    q_all = q_ref[...]
+    gt[0] = square(jnp.concatenate([q_all, q_all], axis=0))
     pl.semaphore_wait(barrier, W - 1 + N - 1)
 
-    for t in range(PARTS):
-        hop_x(t).start()
-        hop_c(t).start()
-
-        @pl.when(e == 0)
-        def _():
-            hop_a(t).start()
-
-    lv[0, nar] = pairs_ref[...]
     for d in range(1, N):
         list_near(d).start()
-    q_all = q_ref[...]
-    gt[0] = square(jnp.concatenate([q_all, q_all], axis=0))
     gram_send(0)
+    hop_c(0).start()
+    hop_x(0).start()
+    for d in range(1, N):
+        place = lv.at[0, behind(d)]
+        remote(place, place, "ln", d, nearby(d)).wait_recv()
+    for d in range(1, 4):
+        list_wide(d).start()
+    for t in range(1, PARTS):
+        hop_c(t).start()
+        hop_x(t).start()
+
+    @pl.when(e == 0)
+    def _():
+        for t in range(PARTS):
+            hop_a(t).start()
+
+    def relay_x(t):
+        hop_x(t).wait_recv()
+
+        @pl.when(e == 1)
+        def _():
+            hop_a(t, 1).start()
+
+    def relay_c(t):
+        hop_c(t).wait_recv()
+        hop_f(t).start()
+
     lax.fori_loop(0, B, normalise, 0, unroll=2)
 
     def places(rows, columns, of):
@@ -603,12 +622,7 @@
             BS, BS, lambda l: ((l // QR + N - a) & (N - 1)) * QR + (l & (QR - 1))
         )
 
-    for d in range(1, N):
-        place = lv.at[0, behind(d)]
-        remote(place, place, "ln", d, nearby(d)).wait_recv()
-    for d in range(1, 4):
-        list_wide(d).start()
-
+    relay_x(0)
     for jq in range(JQ):
         value = jnp.zeros((R, BS), jnp.float32)
         for s in range(N):
@@ -617,6 +631,8 @@
             value = jnp.where(slot_is(s), one, value)
         wp[:, jq * BS : (jq + 1) * BS] = value
 
+    relay_x(1)
+    relay_c(0)
     for d in range(1, W):
         gram_wide_in(0, d).wait_recv()
     _, _, inverse0 = factor_of(gram_value(0)[:R, :R], R)
@@ -639,7 +655,7 @@
             vec_wide(k, d).start()
 
     vec_send(0, qc)
-
+    relay_x(2)
     for d in range(1, 4):
         remote(lv.at[d], lv.at[d], "lw", d, wide(DST[d])).wait_recv()
     local = pltpu.make_async_copy(lv, ls, sem["m_ls"])
@@ -661,11 +677,11 @@
             vj = jnp.zeros((8, BS), jnp.int32)
             for c in range(C):
                 if kind == 0:
-                    i = ls[0, mq, 0, other * C + c]
-                    j = ls[0, mq, 0, HALF + other * C + c]
+                    i = lax.rem(ls[0, mq, 0, other * C + c], B)
+                    j = lax.rem(ls[0, mq, 0, HALF + other * C + c], B)
                 else:
-                    j = ls[s - 1, mq, 0, me * C + c]
-                    i = ls[s - 1, mq, 0, HALF + me * C + c]
+                    j = lax.rem(ls[s - 1, mq, 0, me * C + c], B)
+                    i = lax.rem(ls[s - 1, mq, 0, HALF + me * C + c], B)
                 idx_i[ch * C + c] = i
                 idx_j[ch * C + c] = j
                 vi = jnp.where(sub8 == c, i, vi)
@@ -680,6 +696,8 @@
 
         lax.fori_loop(0, N, indices, 0)
 
+    relay_x(3)
+    relay_c(1)
     turned = jnp.transpose(oht1[...])[: oh1.shape[0]].astype(jnp.bfloat16)
     oh1[...] = jnp.concatenate([turned, turned], axis=1)
     turned = jnp.transpose(oht2[...])[: oh2.shape[0]].astype(jnp.bfloat16)
@@ -704,16 +722,9 @@
             lax.fori_loop(0, N, make, 0)
 
     tiles_of(0)
-    for t in range(PARTS):
-        hop_x(t).wait_recv()
-
-        @pl.when(e == 1)
-        def _():
-            hop_a(t, 1).start()
-
-        hop_c(t).wait_recv()
-        hop_f(t).start()
+    relay_c(2)
     tiles_of(1)
+    relay_c(3)
     tiles_of(2)
     for t in range(PARTS):
         hop_a(t).wait_recv()
@@ -789,7 +800,7 @@
                 tf2[pl.ds(pl.multiple_of((ch * C + c) * R, R), R), :] = value
             return carry
 
-        lax.fori_loop(0, chunks, second, 0, unroll=2)
+        lax.fori_loop(0, chunks, second, 0, unroll=4)
 
         def keep2(r, value):
             for a in range(N):
@@ -835,7 +846,7 @@
                     )
                 return carry
 
-            lax.fori_loop(first_chunk, first_chunk + slots_of_chunk.count(s), first, 0, unroll=2)
+            lax.fori_loop(first_chunk, first_chunk + slots_of_chunk.count(s), first, 0, unroll=4)
 
         def keep1(r, value):
             for s in range(N):
@@ -983,7 +994,7 @@
         scratch_shapes=scratch,
         compiler_params=pltpu.CompilerParams(collective_id=1, has_side_effects=True),
         name="fused",
-    )(points, q_init, lax.rem(pairs, B).reshape(1, 2 * pair_count))
+    )(points, q_init, pairs.reshape(1, 2 * pair_count))
 
 
 def lanczos(first, local, owners, tiles, q_init, wide_count, narrow_count, total):

time: 135 us -> 112 us (0.83)
  Pallas kernels: 129 us -> 107 us
    pallas_call x1, Pallas kernels: 129 us -> 107 us  [fused(): pl.pallas_call(functools.partial(fused_kernel, dims, tuple(names)), out_s...]
where the time goes in v2:
time: 112 us
  Pallas kernels  107 us (96%)
  local copies, waits for them, and re-layouts  4.36 us (4%)
    pallas_call x1, Pallas kernels, fused(): pl.pallas_call(functools.partial(fused_kernel, dims, tuple(names)), out_s...  107 us
    unnamed x2, local copies, waits for them, and re-layouts  3.09 us

profile of v2, /device:TPU:0, one launch (start us, length us, event | category | flops | bytes accessed | tf_op | source)
XLA Modules:
  0.0 111.6 jit_solution(16954188757896872782)
XLA Ops:
  0.6 1.3 %reshape.7.pairs_ref = s32[1,128]{1,0:T(1,128)} reshape(s32[2,64]{1,0:T(2,128)} %param.5) | data formatting | bytes 1024 | tf_op jit(solution)/shard_map/reshape | solution.py:997
  1.9 106.6 %fused.1 = (f32[16,4096]{1,0:T(8,128)}, f32[3,2,16,16]{3,2,1,0:T(8,128)}) custom-call(bf16[4096,256]{1,0:T(8,128)(2,1)} %points.1, f32[16,4096]{1,0:T(8,128)} %q_ref.1, s32[1,128]{1,0:T(1,128)} %reshape.7.pairs_ref), custom_call_target="tpu_custom_call" | custom-call | tf_op jit(solution)/shard_map/fused/pallas_call | solution.py:986
  108.5 1.7 %copy.7 = f32[16,4096]{1,0:T(8,128)} copy(f32[16,4096]{1,0:T(8,128)} %get-tuple-element.4) | data formatting | bytes 524288
  110.2 1.4 %copy.8 = f32[3,2,16,16]{3,2,1,0:T(8,128)} copy(f32[3,2,16,16]{3,2,1,0:T(8,128)} %get-tuple-element.5) | data formatting | bytes 12288

commit v3 on v2

--- a/solution.py
+++ b/solution.py
@@ -396,8 +396,8 @@
 def fused_kernel(dims, names, points, q_ref, pairs_ref, out, coef, *refs):
     W, N, C, R, B, F, total = dims
     s_ = dict(zip(names, refs))
-    (unit, uq0, uq1, uq2, uq3, uq4, kt, tf1, tf2, vo, vr, rep, perm, shift, yt, zt, oht1, oht2, oh1, oh2, lv, ls, idx_i, idx_j, n2, w2, o1n, o1w, i1n, i1w,
-     y1, y2, gs, gn, gt, gw, fin, qc, pv, wp, zp, at, inv, up) = (s_[n] for n in DATA)
+    (unit, uq0, uq1, uq2, uq3, uq4, kt, tf1, tf2, vo, vr, rep, perm, shift, yt, zt, oht1, oht2, oh1, oh2, lv, ls, idx_i, idx_j, idx_v, n2, w2, o1n, o1w, i1n, i1w,
+     y1, y2, gs, gn, gt, gw, qc, pv, wp, zp, at, inv, up) = (s_[n] for n in DATA)
     sem = s_
     uq = (uq0, uq1, uq2, uq3, uq4)
     QR = BS // N
@@ -496,13 +496,6 @@
         place = gw.at[k, lax.rem(me - d + W, W)]
         return remote(place, place, "gw", (k, d), wide(lax.rem(me + d, W)))
 
-    def fin_near(d):
-        return remote(fin.at[nar], fin.at[nar], "fn", d, nearby(d))
-
-    def fin_near_in(d):
-        place = fin.at[behind(d)]
-        return remote(place, place, "fn", d, nearby(d))
-
     barrier = pltpu.get_barrier_semaphore()
     for d in range(1, W):
         pl.semaphore_signal(barrier, inc=1, device_id=wide(lax.rem(me + d, W)), device_id_type=MESH)
@@ -631,8 +624,6 @@
             value = jnp.where(slot_is(s), one, value)
         wp[:, jq * BS : (jq + 1) * BS] = value
 
-    relay_x(1)
-    relay_c(0)
     for d in range(1, W):
         gram_wide_in(0, d).wait_recv()
     _, _, inverse0 = factor_of(gram_value(0)[:R, :R], R)
@@ -655,7 +646,8 @@
             vec_wide(k, d).start()
 
     vec_send(0, qc)
-    relay_x(2)
+    relay_x(1)
+    relay_c(0)
     for d in range(1, 4):
         remote(lv.at[d], lv.at[d], "lw", d, wide(DST[d])).wait_recv()
     local = pltpu.make_async_copy(lv, ls, sem["m_ls"])
@@ -684,6 +676,7 @@
                     i = lax.rem(ls[s - 1, mq, 0, HALF + me * C + c], B)
                 idx_i[ch * C + c] = i
                 idx_j[ch * C + c] = j
+                idx_v[ch * C + c] = s * B + j
                 vi = jnp.where(sub8 == c, i, vi)
                 vj = jnp.where(sub8 == c, j, vj)
             rows = pl.ds(pl.multiple_of(ch * C, C), C)
@@ -696,7 +689,7 @@
 
         lax.fori_loop(0, N, indices, 0)
 
-    relay_x(3)
+    relay_x(2)
     relay_c(1)
     turned = jnp.transpose(oht1[...])[: oh1.shape[0]].astype(jnp.bfloat16)
     oh1[...] = jnp.concatenate([turned, turned], axis=1)
@@ -719,9 +712,10 @@
                     kt[rows, BS:] = low
                 return carry
 
-            lax.fori_loop(0, N, make, 0)
+            lax.fori_loop(0, N, make, 0, unroll=2)
 
     tiles_of(0)
+    relay_x(3)
     relay_c(2)
     tiles_of(1)
     relay_c(3)
@@ -734,7 +728,6 @@
     tiles_of(3)
 
     chunks = len(kinds) * N
-    slots_of_chunk = [s for s, _ in kinds for _ in range(N)]
 
     def unpacked(ref, k, d):
         scale = quarter_scale(ref[k, d, JQ * R : (JQ + 1) * R, :].astype(jnp.int32)) * (1.0 / LEVELS)
@@ -800,7 +793,7 @@
                 tf2[pl.ds(pl.multiple_of((ch * C + c) * R, R), R), :] = value
             return carry
 
-        lax.fori_loop(0, chunks, second, 0, unroll=4)
+        lax.fori_loop(0, chunks, second, 0, unroll=8)
 
         def keep2(r, value):
             for a in range(N):
@@ -825,28 +818,25 @@
             remote(w2.at[k, d], w2.at[k, d], "vw", (k, d), wide(DST[d])).wait_recv()
             keep_remote(d + 1, unpacked(w2, k, d))
 
-        for s in range(SLOTS):
-            first_chunk = slots_of_chunk.index(s)
-
-            def first(ch, carry):
-                left = []
-                for c in range(C):
-                    value = vr[s * B + idx_j[ch * C + c]]
-                    value = jnp.where(slot_is(c % N, lane2), value, jnp.zeros_like(value))
-                    pieces = [jnp.zeros_like(value)] * (C // N)
-                    pieces[c // N] = value
-                    left.append(jnp.concatenate(pieces, axis=1))
-                tile = kt[pl.ds(pl.multiple_of(ch * C * QR, C * QR), C * QR), :]
-                full = jnp.dot(jnp.concatenate(left, axis=0), tile, preferred_element_type=jnp.float32)
-                for c in range(C):
-                    high = full[2 * R * c : 2 * R * c + R]
-                    low = full[2 * R * c + R : 2 * R * (c + 1)]
-                    tf1[pl.ds(pl.multiple_of((ch * C + c) * R, R), R), :] = (
-                        high[:, :BS] + high[:, BS:] + low[:, :BS]
-                    )
-                return carry
-
-            lax.fori_loop(first_chunk, first_chunk + slots_of_chunk.count(s), first, 0, unroll=4)
+        def first(ch, carry):
+            left = []
+            for c in range(C):
+                value = vr[idx_v[ch * C + c]]
+                value = jnp.where(slot_is(c % N, lane2), value, jnp.zeros_like(value))
+                pieces = [jnp.zeros_like(value)] * (C // N)
+                pieces[c // N] = value
+                left.append(jnp.concatenate(pieces, axis=1))
+            tile = kt[pl.ds(pl.multiple_of(ch * C * QR, C * QR), C * QR), :]
+            full = jnp.dot(jnp.concatenate(left, axis=0), tile, preferred_element_type=jnp.float32)
+            for c in range(C):
+                high = full[2 * R * c : 2 * R * c + R]
+                low = full[2 * R * c + R : 2 * R * (c + 1)]
+                tf1[pl.ds(pl.multiple_of((ch * C + c) * R, R), R), :] = (
+                    high[:, :BS] + high[:, BS:] + low[:, :BS]
+                )
+            return carry
+
+        lax.fori_loop(0, chunks, first, 0, unroll=8)
 
         def keep1(r, value):
             for s in range(N):
@@ -891,13 +881,14 @@
     lax.fori_loop(0, STEPS, step, 0)
     gram_collect(STEPS)
     gram_finish(STEPS)
-    for jq, value in enumerate(lanes_of(qc)):
-        fin[nar, jq * R : (jq + 1) * R, :] = value
+    for jq, value in enumerate(packed(lanes_of(qc))):
+        n2[STEPS, nar, jq * R : (jq + 1) * R, :] = value
     for d in range(1, N):
-        fin_near(d).start()
+        vec_near(STEPS, d).start()
     for d in range(1, N):
-        fin_near_in(d).wait_recv()
-    value = moved(jnp.concatenate([fin[q] for q in range(N)], axis=1), perm)
+        vec_near_in(STEPS, d).wait_recv()
+    pieces = [jnp.concatenate(unpacked(n2, STEPS, q), axis=0) for q in range(N)]
+    value = moved(jnp.concatenate(pieces, axis=1), perm)
     for jq in range(JQ):
         for s in range(N):
             b = jq * N + s
@@ -910,7 +901,7 @@
         hop_f(t).wait_send()
     for d in range(1, N):
         list_near(d).wait_send()
-        fin_near(d).wait_send()
+        vec_near(STEPS, d).wait_send()
     for d in range(1, 4):
         list_wide(d).wait_send()
     for d in range(1, W):
@@ -929,8 +920,8 @@
 
 DATA = (
     "unit", "uq0", "uq1", "uq2", "uq3", "uq4", "kt", "tf1", "tf2", "vo", "vr", "rep", "perm", "shift", "yt", "zt", "oht1", "oht2",
-    "oh1", "oh2", "lv", "ls", "idx_i", "idx_j", "n2", "w2", "o1n", "o1w", "i1n", "i1w", "y1", "y2",
-    "gs", "gn", "gt", "gw", "fin", "qc", "pv", "wp", "zp", "at", "inv", "up",
+    "oh1", "oh2", "lv", "ls", "idx_i", "idx_j", "idx_v", "n2", "w2", "o1n", "o1w", "i1n", "i1w", "y1", "y2",
+    "gs", "gn", "gt", "gw", "qc", "pv", "wp", "zp", "at", "inv", "up",
 )
 
 
@@ -957,21 +948,21 @@
         "oh1": V((B, 2 * P_), bf16), "oh2": V((N * Z_ROWS, 2 * P_), bf16),
         "lv": V((4, N, 1, 2 * pair_count), i32), "ls": pltpu.SMEM((4, N, 1, 2 * pair_count), i32),
         "idx_i": pltpu.SMEM((P_,), i32), "idx_j": pltpu.SMEM((P_,), i32),
-        "n2": V((STEPS, N) + message, i16), "w2": V((STEPS, 4) + message, i16),
+        "idx_v": pltpu.SMEM((P_,), i32),
+        "n2": V((rounds, N) + message, i16), "w2": V((STEPS, 4) + message, i16),
         "o1n": V((STEPS, N) + message, i16), "o1w": V((STEPS, 4) + message, i16),
         "i1n": V((STEPS, N) + message, i16), "i1w": V((STEPS, 4) + message, i16),
         "y1": V((N, JQ * R, BS), f32), "y2": V((SLOTS, JQ * R, BS), f32),
         "gs": V((rounds, 8, BS), f32), "gn": V((rounds, N, 8, BS), f32),
         "gt": V((rounds, 8, BS), f32), "gw": V((rounds, W, 8, BS), f32),
-        "fin": V((N, JQ * R, BS), f32),
         "qc": V((R, columns), f32), "pv": V((R, columns), f32), "wp": V((R, columns), f32),
         "zp": V((R, columns), f32),
         "at": V((R, R), f32), "inv": V((R, R), f32), "up": V((R, R), f32),
     }
     sems = {
         "px": (PARTS,), "pc": (PARTS,), "pf": (PARTS,), "pa": (PARTS,), "ln": (N,), "lw": (4,),
-        "vn": (STEPS, N), "vw": (STEPS, 4), "sn": (STEPS, N), "sw": (STEPS, 4),
-        "gn": (rounds, N), "gw": (rounds, W), "fn": (N,),
+        "vn": (rounds, N), "vw": (STEPS, 4), "sn": (STEPS, N), "sw": (STEPS, 4),
+        "gn": (rounds, N), "gw": (rounds, W),
     }
     names = list(DATA)
     scratch = [shapes[n] for n in DATA]

time: 112 us -> 107 us (0.955)
  Pallas kernels: 107 us -> 102 us
    pallas_call x1, Pallas kernels: 107 us -> 102 us  [fused(): pl.pallas_call(functools.partial(fused_kernel, dims, tuple(names)), out_s...]
where the time goes in v3:
time: 107 us
  Pallas kernels  102 us (95%)
  local copies, waits for them, and re-layouts  4.36 us (4%)
    pallas_call x1, Pallas kernels, fused(): pl.pallas_call(functools.partial(fused_kernel, dims, tuple(names)), out_s...  102 us
    unnamed x2, local copies, waits for them, and re-layouts  3.09 us

profile of v3, /device:TPU:0, one launch (start us, length us, event | category | flops | bytes accessed | tf_op | source)
XLA Modules:
  0.0 106.9 jit_solution(9959228559518682307)
XLA Ops:
  0.6 1.3 %reshape.7.pairs_ref = s32[1,128]{1,0:T(1,128)} reshape(s32[2,64]{1,0:T(2,128)} %param.5) | data formatting | bytes 1024 | tf_op jit(solution)/shard_map/reshape | solution.py:988
  1.9 101.9 %fused.1 = (f32[16,4096]{1,0:T(8,128)}, f32[3,2,16,16]{3,2,1,0:T(8,128)}) custom-call(bf16[4096,256]{1,0:T(8,128)(2,1)} %points.1, f32[16,4096]{1,0:T(8,128)} %q_ref.1, s32[1,128]{1,0:T(1,128)} %reshape.7.pairs_ref), custom_call_target="tpu_custom_call" | custom-call | tf_op jit(solution)/shard_map/fused/pallas_call | solution.py:977
  103.8 1.7 %copy.7 = f32[16,4096]{1,0:T(8,128)} copy(f32[16,4096]{1,0:T(8,128)} %get-tuple-element.4) | data formatting | bytes 524288
  105.4 1.4 %copy.8 = f32[3,2,16,16]{3,2,1,0:T(8,128)} copy(f32[3,2,16,16]{3,2,1,0:T(8,128)} %get-tuple-element.5) | data formatting | bytes 12288

commit v4 on v3

--- a/solution.py
+++ b/solution.py
@@ -393,12 +393,14 @@
 PARTS = 4
 
 
-def fused_kernel(dims, names, points, q_ref, pairs_ref, out, coef, *refs):
+def fused_kernel(dims, names, points_ref, q_ref, pairs_ref, out, coef, *refs):
     W, N, C, R, B, F, total = dims
     s_ = dict(zip(names, refs))
-    (unit, uq0, uq1, uq2, uq3, uq4, kt, tf1, tf2, vo, vr, rep, perm, shift, yt, zt, oht1, oht2, oh1, oh2, lv, ls, idx_i, idx_j, idx_v, n2, w2, o1n, o1w, i1n, i1w,
+    (points, unit, uq0, uq1, uq2, uq3, uq4, kt, tf1, tf2, vo, vr, rep, perm, shift, yt, zt, oht1, oht2, oh1, oh2, lv, ls, idx_i, idx_j, idx_v, n2, w2, o1n, o1w, i1n, i1w,
      y1, y2, gs, gn, gt, gw, qc, pv, wp, zp, at, inv, up) = (s_[n] for n in DATA)
     sem = s_
+    taken = pltpu.make_async_copy(points_ref, points, sem["m_points"])
+    taken.start()
     uq = (uq0, uq1, uq2, uq3, uq4)
     QR = BS // N
     JQ = B // N
@@ -510,7 +512,6 @@
         uq0[b] = unit_rows(points[pl.ds(pl.multiple_of(b * BS + nar * QR, QR), QR), :])
         return carry
 
-    lax.fori_loop(0, B, quarter, 0, unroll=4)
 
     def square(x_):
         four = jnp.concatenate([x_] * (BS // (2 * R)), axis=0)
@@ -567,6 +568,8 @@
     lv[0, nar] = pairs_ref[...]
     q_all = q_ref[...]
     gt[0] = square(jnp.concatenate([q_all, q_all], axis=0))
+    taken.wait()
+    lax.fori_loop(0, B, quarter, 0, unroll=4)
     pl.semaphore_wait(barrier, W - 1 + N - 1)
 
     for d in range(1, N):
@@ -642,6 +645,8 @@
             n2[k, nar, jq * R : (jq + 1) * R, :] = value
         for d in range(1, N):
             vec_near(k, d).start()
+
+    def vec_far(k):
         for d in range(4):
             vec_wide(k, d).start()
 
@@ -719,6 +724,7 @@
     relay_c(2)
     tiles_of(1)
     relay_c(3)
+    vec_far(0)
     tiles_of(2)
     for t in range(PARTS):
         hop_a(t).wait_recv()
@@ -873,6 +879,7 @@
         @pl.when(k < STEPS - 1)
         def _():
             vec_send(k + 1, wp)
+            vec_far(k + 1)
 
         gram_start(k + 1)
         return carry
@@ -919,7 +926,7 @@
 
 
 DATA = (
-    "unit", "uq0", "uq1", "uq2", "uq3", "uq4", "kt", "tf1", "tf2", "vo", "vr", "rep", "perm", "shift", "yt", "zt", "oht1", "oht2",
+    "points", "unit", "uq0", "uq1", "uq2", "uq3", "uq4", "kt", "tf1", "tf2", "vo", "vr", "rep", "perm", "shift", "yt", "zt", "oht1", "oht2",
     "oh1", "oh2", "lv", "ls", "idx_i", "idx_j", "idx_v", "n2", "w2", "o1n", "o1w", "i1n", "i1w", "y1", "y2",
     "gs", "gn", "gt", "gw", "qc", "pv", "wp", "zp", "at", "inv", "up",
 )
@@ -939,7 +946,7 @@
     rounds = STEPS + 1
     columns = JQ * BS
     shapes = {
-        "unit": V((B, BS, F), bf16), **{f"uq{s}": V((B, QR, F), bf16) for s in range(SLOTS)}, "kt": V((P_ * QR, 2 * BS), bf16),
+        "points": V(points.shape, bf16), "unit": V((B, BS, F), bf16), **{f"uq{s}": V((B, QR, F), bf16) for s in range(SLOTS)}, "kt": V((P_ * QR, 2 * BS), bf16),
         "tf1": V((P_ * R, BS), f32), "tf2": V((P_ * R, BS), f32),
         "vo": V((B, 2 * R, BS), bf16), "vr": V((SLOTS * B, 2 * R, BS), bf16),
         "oht1": V((P_, BS), f32), "oht2": V((P_, 2 * BS), f32),
@@ -970,8 +977,9 @@
         for way in "sr":
             names.append(way + "_" + name)
             scratch.append(pltpu.SemaphoreType.DMA(shape))
-    names.append("m_ls")
-    scratch.append(pltpu.SemaphoreType.DMA)
+    for name in ("m_ls", "m_points"):
+        names.append(name)
+        scratch.append(pltpu.SemaphoreType.DMA)
     vmem = pl.BlockSpec(memory_space=pltpu.VMEM)
     dims = (W, N, C, R, B, F, B * BS * W)
     return pl.pallas_call(
@@ -980,7 +988,7 @@
             jax.ShapeDtypeStruct((R, cols), f32),
             jax.ShapeDtypeStruct((STEPS, 2, R, R), f32),
         ),
-        in_specs=[vmem, vmem, vmem],
+        in_specs=[pl.BlockSpec(memory_space=pl.ANY), vmem, vmem],
         out_specs=(vmem, vmem),
         scratch_shapes=scratch,
         compiler_params=pltpu.CompilerParams(collective_id=1, has_side_effects=True),

time: 107 us -> 107 us (level)
  no operation moved by 1% of the time
where the time goes in v4:
time: 107 us
  Pallas kernels  102 us (95%)
  local copies, waits for them, and re-layouts  4.36 us (4%)
    pallas_call x1, Pallas kernels, fused(): pl.pallas_call(functools.partial(fused_kernel, dims, tuple(names)), out_s...  102 us
    unnamed x2, local copies, waits for them, and re-layouts  3.09 us

profile of v4, /device:TPU:0, one launch (start us, length us, event | category | flops | bytes accessed | tf_op | source)
XLA Modules:
  0.0 106.8 jit_solution(11218955391343184148)
XLA Ops:
  0.6 1.3 %reshape.7.pairs_ref = s32[1,128]{1,0:T(1,128)} reshape(s32[2,64]{1,0:T(2,128)} %param.5) | data formatting | bytes 1024 | tf_op jit(solution)/shard_map/reshape | solution.py:996
  1.9 101.8 %fused.1 = (f32[16,4096]{1,0:T(8,128)}, f32[3,2,16,16]{3,2,1,0:T(8,128)}) custom-call(bf16[4096,256]{1,0:T(8,128)(2,1)} %points_ref.1, f32[16,4096]{1,0:T(8,128)} %q_ref.1, s32[1,128]{1,0:T(1,128)} %reshape.7.pairs_ref), custom_call_target="tpu_custom_call" | custom-call | tf_op jit(solution)/shard_map/fused/pallas_call | solution.py:985
  103.7 1.7 %copy.7 = f32[16,4096]{1,0:T(8,128)} copy(f32[16,4096]{1,0:T(8,128)} %get-tuple-element.4) | data formatting | bytes 524288
  105.4 1.4 %copy.8 = f32[3,2,16,16]{3,2,1,0:T(8,128)} copy(f32[3,2,16,16]{3,2,1,0:T(8,128)} %get-tuple-element.5) | data formatting | bytes 12288
